TPU v7x, 128 devices: a whole 4x4x4 slice. The times are simulated.
128 devices in a mesh: grp: 2 (over y_hi), lat: 4 (over z), lon: 16 (over y_lo, x, core).
Axes of the slice: x: 4, y: 4 (y_hi: 2, y_lo: 2; y = y_hi * 2 + y_lo), z: 4, core: 2. Of those that a mesh axis runs over, the one named last changes fastest.
Arguments:
- state: bfloat16 [2, 64, 2048, 512], P('grp', 'lat', 'lon'), may hold values from -6 to 6
- intersection_lists: int32 [2, 4, 16, 3, 64], P('grp', 'lat', 'lon'), may hold values from 0 to 63, as said below
- intersection_matrices: bfloat16 [2, 4, 16, 64, 128, 128], P('grp', 'lat', 'lon'), may hold values from -0.5 to 0.5
- water_indicator: int32 [64, 4096], P('lat', 'lon'), may hold values from 0 to 1, as said below
- atmosphere_kernels: bfloat16 [2, 3, 3, 512, 512], replicated, may hold values from -0.09375 to 0.09375
- ocean_kernels: bfloat16 [2, 3, 3, 256, 256], replicated, may hold values from -0.125 to 0.125
- flux_projection: bfloat16 [512, 256], replicated, may hold values from -0.25 to 0.25
- coupling_matrix: bfloat16 [256, 512], replicated, may hold values from -0.375 to 0.375
Outputs:
- new_state: bfloat16 [2, 64, 2048, 512], P('grp', 'lat', 'lon')
Inputs may be any that keep to these rules, and one draw needn't show every extreme that they name: intersection_lists[g, i, j] lists the 64 intersections whose source block lies on tile (i, j) of component g (0 atmosphere, 1 ocean). Row 0 is the tile number of the receiving tile of the other component; row 1 the source block, below 16 for atmosphere sources and below 32 for ocean sources; row 2 the receiving block, below 32 on ocean tiles and below 16 on atmosphere tiles. A source tile names one receiving tile at most 2 times, and every source tile names some receiving tile exactly 2 times. `water_indicator`: the share of land differs from tile to tile.
All inputs are finite; a program needn't handle non-finite values.
Results may differ from a plain program's by a relative error of at most 0.01.
Values may be sent and summed in bfloat16 or wider, within the bound.
A program may use at most 192 MiB of HBM per device.

v0:
```python
from functools import partial

import jax
import jax.numpy as jnp
from jax import lax
from jax.sharding import PartitionSpec as P

LAYERS = 2
PATCH_PARALLELS = 8
PATCH_MERIDIANS = 16
SLOTS = 2


def extended(block, sides, width, periodic):
    for axis, dim in sides:
        count = lax.axis_size(axis)
        forward = [(i, i + 1) for i in range(count - 1)]
        if periodic:
            forward.append((count - 1, 0))
        backward = [(target, source) for source, target in forward]
        low = lax.ppermute(
            lax.slice_in_dim(block, block.shape[dim] - width, None, axis=dim), axis, forward
        )
        high = lax.ppermute(lax.slice_in_dim(block, 0, width, axis=dim), axis, backward)
        block = jnp.concatenate([low, block, high], axis=dim)
    return block


def partner(value, axis, bit):
    mask = 2**bit
    pairs = [(source, source ^ mask) for source in range(lax.axis_size(axis))]
    return lax.ppermute(value, axis, pairs)


def tile_blocks(grid_field, block_rows, block_cols):
    patch_span_down, patch_span_across, channels = grid_field.shape
    reshaped = grid_field.reshape(
        patch_span_down // block_rows,
        block_rows,
        patch_span_across // block_cols,
        block_cols,
        channels,
    )
    return reshaped.transpose(0, 2, 1, 3, 4).reshape(-1, block_rows * block_cols, channels)


def panel_values(blocks, patch_span_down, patch_span_across, block_rows, block_cols):
    channels = blocks.shape[-1]
    reshaped = blocks.reshape(
        patch_span_down // block_rows,
        patch_span_across // block_cols,
        block_rows,
        block_cols,
        channels,
    )
    return reshaped.transpose(0, 2, 1, 3, 4).reshape(patch_span_down, patch_span_across, channels)


def shifted_conv(padded, kernel, patch_span_down, patch_span_across):
    patch_totals = jnp.zeros((patch_span_down * patch_span_across, kernel.shape[3]), jnp.float32)
    for shift_row in range(3):
        for shift_col in range(3):
            window = padded[
                shift_row : shift_row + patch_span_down, shift_col : shift_col + patch_span_across
            ].reshape(patch_span_down * patch_span_across, -1)
            patch_totals = patch_totals + jnp.dot(
                window, kernel[shift_row, shift_col], preferred_element_type=jnp.float32
            )
    return patch_totals.reshape(patch_span_down, patch_span_across, -1)


def atmos_conv(padded, kernel):
    return shifted_conv(padded, kernel, padded.shape[0] - 2, padded.shape[1] - 2)


def ocean_conv(padded, kernel):
    patch_span_down = padded.shape[0] - 2
    patch_span_across = padded.shape[1] - 2
    channels = kernel.shape[2]
    ocean_cells = padded.reshape(patch_span_down + 2, 2 * patch_span_across + 4, channels)[
        :, 1 : 2 * patch_span_across + 3
    ]
    mixed = shifted_conv(ocean_cells, kernel, patch_span_down, 2 * patch_span_across)
    return mixed.reshape(patch_span_down, patch_span_across, 2 * channels)


def rims(hidden):
    widened = extended(hidden, (("lon", 1),), 1, True)
    return extended(widened, (("lat", 0),), 1, False)


def cross(parcel):
    return partner((parcel[0], parcel[1]), "grp", 0)


def within(parcel):
    values, labels = parcel
    return (
        lax.all_to_all(values, ("lat", "lon"), split_axis=0, concat_axis=0, tiled=True),
        lax.all_to_all(labels, ("lat", "lon"), split_axis=0, concat_axis=0, tiled=True),
    )


def pack_slots(payload, owners, targets, tile_count):
    entries = payload.shape[0]
    owner_hits = (owners[:, None] == jnp.arange(tile_count)[None, :]).astype(jnp.int32)
    earlier = jnp.cumsum(owner_hits, axis=0) - owner_hits
    slot_rank = jnp.sum(earlier * owner_hits, axis=1)
    slot_index = owners * SLOTS + slot_rank
    placing = jnp.arange(tile_count * SLOTS)[:, None] == slot_index[None, :]
    outgoing = jnp.dot(
        placing.astype(jnp.bfloat16),
        payload.reshape(entries, -1),
        preferred_element_type=jnp.float32,
    )
    outgoing = outgoing.astype(jnp.bfloat16).reshape((tile_count * SLOTS,) + payload.shape[1:])
    labels = jnp.sum(placing.astype(jnp.int32) * (targets[None, :] + 1), axis=1) - 1
    return (outgoing, labels)


def body(
    state,
    intersection_lists,
    intersection_matrices,
    water_indicator,
    atmosphere_kernels,
    ocean_kernels,
    flux_projection,
    coupling_matrix,
):
    current = state[0]
    patch_span_down, patch_span_across, width_a = current.shape
    marine_meridians = width_a // 2
    block_extent = PATCH_PARALLELS * PATCH_MERIDIANS
    is_ocean = lax.axis_index("grp") == 1
    tile_count = lax.axis_size("lat") * lax.axis_size("lon")
    entries = intersection_lists.shape[-1]
    label_lookup = intersection_lists.reshape(3, entries)
    owners, sources, targets = (label_lookup[0], label_lookup[1], label_lookup[2])
    remapping_factors = intersection_matrices.reshape(entries, block_extent, block_extent)
    mask_bf = water_indicator.astype(jnp.bfloat16)

    def atmos_source(grid_state):
        flux = jnp.dot(
            grid_state.reshape(-1, width_a), flux_projection, preferred_element_type=jnp.float32
        )
        flux = flux.astype(jnp.bfloat16).reshape(
            patch_span_down, patch_span_across, marine_meridians
        )
        return tile_blocks(flux, PATCH_PARALLELS, PATCH_MERIDIANS)[sources]

    def ocean_source(grid_state):
        surface = (
            grid_state.reshape(patch_span_down, 2 * patch_span_across, marine_meridians)
            * mask_bf[:, :, None]
        )
        return tile_blocks(surface, PATCH_PARALLELS, PATCH_MERIDIANS)[sources]

    chosen = lax.cond(is_ocean, ocean_source, atmos_source, current)
    payload = jnp.einsum(
        "eij,ejk->eik", remapping_factors, chosen, preferred_element_type=jnp.float32
    ).astype(jnp.bfloat16)
    arrived = within(cross(pack_slots(payload, owners, targets, tile_count)))

    def atmos_sink(received):
        values, marks = received
        entry_count = patch_span_down * patch_span_across // block_extent
        selector = (jnp.arange(entry_count)[:, None] == marks[None, :]).astype(jnp.bfloat16)
        patch_totals = jnp.dot(
            selector, values.reshape(values.shape[0], -1), preferred_element_type=jnp.float32
        )
        skin_warmth_given = patch_totals.astype(jnp.bfloat16).reshape(
            entry_count, block_extent, marine_meridians
        )
        skin_warmth_given = panel_values(
            skin_warmth_given, patch_span_down, patch_span_across, PATCH_PARALLELS, PATCH_MERIDIANS
        )
        surface_forcing = jnp.dot(
            skin_warmth_given.reshape(-1, marine_meridians),
            coupling_matrix,
            preferred_element_type=jnp.float32,
        )
        return surface_forcing.reshape(patch_span_down, patch_span_across, width_a)

    def ocean_sink(received):
        values, marks = received
        entry_count = 2 * patch_span_down * patch_span_across // block_extent
        selector = (jnp.arange(entry_count)[:, None] == marks[None, :]).astype(jnp.bfloat16)
        patch_totals = jnp.dot(
            selector, values.reshape(values.shape[0], -1), preferred_element_type=jnp.float32
        )
        patch_totals = panel_values(
            patch_totals.reshape(entry_count, block_extent, marine_meridians),
            patch_span_down,
            2 * patch_span_across,
            PATCH_PARALLELS,
            PATCH_MERIDIANS,
        )
        return patch_totals.reshape(patch_span_down, patch_span_across, width_a)

    ocean_mask = jnp.broadcast_to(
        water_indicator.astype(jnp.float32)[:, :, None],
        (patch_span_down, 2 * patch_span_across, marine_meridians),
    )
    multiplier = jnp.where(
        is_ocean, ocean_mask.reshape(patch_span_down, patch_span_across, width_a), 1.0
    )
    for layer_index in range(LAYERS):
        hidden = jax.nn.silu(current.astype(jnp.float32)).astype(jnp.bfloat16)
        padded = rims(hidden)
        mixed = lax.cond(
            is_ocean,
            partial(ocean_conv, kernel=ocean_kernels[layer_index]),
            partial(atmos_conv, kernel=atmosphere_kernels[layer_index]),
            padded,
        )
        update = current.astype(jnp.float32) + mixed
        if layer_index == 0:
            update = update + lax.cond(is_ocean, ocean_sink, atmos_sink, arrived)
        current = (update * multiplier).astype(jnp.bfloat16)
    return current[None]


def solution(mesh):
    placed = (
        P("grp", "lat", "lon", None),
        P("grp", "lat", "lon", None, None),
        P("grp", "lat", "lon", None, None, None),
        P("lat", "lon"),
        P(),
        P(),
        P(),
        P(),
    )
    return jax.shard_map(
        body, mesh=mesh, in_specs=placed, out_specs=P("grp", "lat", "lon", None), check_vma=False
    )
```

profile of v0, /device:TPU:32, one launch (start us, length us, event | category | flops | bytes accessed | tf_op | source)
XLA Modules:
  0.0 525.4 jit_solution(10798559198004612721)
XLA Ops:
  0.0 0.8 slice_bitcast_fusion.76
  0.8 0.7 convert_element_type.62
  1.9 0.7 multiply_add_fusion.1
  2.6 5.3 %conditional.5 = (bf16[64,128,256]{2,1,0:T(8,128)(2,1)}) conditional(s32[]{:T(128)} %convert_element_type.59, (bf16[1,16,128,512]{3,2,1,0:T(8,128)(2,1)}, bf16[512,256]{1,0:T(8,128)(2,1)}, s32[64]{0:T(128)S(1)}) %tuple.31, (bf16[1,16,128,512]{3,2,1,0:T(8,128)(2,1)}, bf16[16,256]{1,0:T(8,128)(2,1)S(1)}, s32[64]{0:T(128)S(1)}) %tuple.32), branch_computations={%region_5.6_spmd, %region_6.7_spmd} | conditional | flops 537396416 | bytes 21001224 | solution.py:159
  2.6 2.3 convolution_convert_fusion.1
  5.0 2.8 gather_fusion.1
  7.9 5.5 %convert_bitcast_fusion = bf16[64,128,256]{1,2,0:T(8,128)(2,1)} fusion(bf16[64,128,256]{2,1,0:T(8,128)(2,1)} %get-tuple-element.159, bf16[1,1,1,64,128,128]{5,4,3,2,1,0:T(8,128)(2,1)S(1)} %copy-done), kind=kOutput, calls=%fused_computation.115 | convolution fusion | flops 538968064 | bytes 10485760 | tf_op jit(solution)/shard_map/eij,ejk->eik/dot_general | solution.py:160
  13.3 6.8 %copy.50 = bf16[8,8,128,256]{3,1,2,0:T(8,128)(2,1)} copy(bf16[8,8,128,256]{2,3,1,0:T(8,128)(2,1)} %bitcast.269) | data formatting | bytes 8388608
  20.1 7.9 %convolution_convert_fusion.2 = bf16[128,32768]{1,0:T(8,128)(2,1)} fusion(bf16[64,32768]{1,0:T(8,128)(2,1)} %bitcast.270, s32[64]{0:T(128)S(1)} %multiply_add_fusion.1), kind=kOutput, calls=%fused_computation.95 | convolution fusion | flops 541073408 | bytes 12583168 | tf_op jit(solution)/shard_map/dot_general | solution.py:111
  28.0 9.1 %copy.51 = bf16[16,8,128,256]{3,2,1,0:T(8,128)(2,1)} copy(bf16[16,8,128,256]{3,1,2,0:T(8,128)(2,1)} %bitcast.261) | data formatting | bytes 16777216
  37.2 10.1 %collective-permute-start.5 = (bf16[128,128,256]{2,1,0:T(8,128)(2,1)}, bf16[128,128,256]{2,1,0:T(8,128)(2,1)}, u32[]{:S(2)}, u32[]{:S(2)}) collective-permute-start(bf16[128,128,256]{2,1,0:T(8,128)(2,1)} %bitcast.291), channel_id=1, source_target_pairs={{0,64},{64,0},{1,65},{65,1},{2,66},{66,2},{3,67},{67,3},{4,68},{68... | collective-permute-start | bytes 25165832 | tf_op jit(solution)/shard_map/ppermute | solution.py:32
  47.4 180.6 %collective-permute-done.4 = s32[128]{0:T(128)S(1)} collective-permute-done((s32[128]{0:T(128)S(1)}, s32[128]{0:T(128)S(1)}, u32[]{:S(2)}, u32[]{:S(2)}) %collective-permute-start.4) | collective-permute-done | bytes 544 | tf_op jit(solution)/shard_map/ppermute | solution.py:32
  228.1 15.4 %all_to_all.17 = s32[64,2,1]{1,2,0:T(1,128)S(1)} all-to-all(s32[64,2,1]{1,2,0:T(1,128)S(1)} %bitcast.311), channel_id=1, replica_groups=mesh['grp'=2,'lat'=4,'lon'=16] {'lat','lon'}, dimensions={0} | all-to-all | bytes 1024 | tf_op jit(solution)/shard_map/all_to_all | solution.py:100
  243.6 7.1 %all-to-all-start.1 = ((bf16[128,128,256]{2,1,0:T(8,128)(2,1)}), bf16[128,128,256]{2,1,0:T(8,128)(2,1)}, u32[]{:S(2)}, u32[]{:S(2)}) async-start(bf16[128,128,256]{2,1,0:T(8,128)(2,1)} %collective-permute-done.5), calls=%async_computation.1 | async-start | bytes 16777216 | tf_op jit(solution)/shard_map/all_to_all | solution.py:99
  250.7 2.8 fusion.34
  253.8 3.7 collective-permute-start.1
  257.5 90.8 %collective-permute-done = bf16[16,1,512]{2,1,0:T(2,128)(2,1)S(1)} collective-permute-done((bf16[16,1,512]{2,1,0:T(2,128)(2,1)S(1)}, bf16[16,1,512]{2,1,0:T(2,128)(2,1)S(1)}, u32[]{:S(2)}, u32[]{:S(2)}) %collective-permute-start) | collective-permute-done | bytes 16416 | tf_op jit(solution)/shard_map/ppermute | solution.py:21
  348.3 1.2 pad_maximum_fusion.2
  349.5 1.3 copy-done.2
  350.9 5.5 %collective-permute-start.2 = (bf16[1,130,512]{2,1,0:T(8,128)(2,1)S(1)}, bf16[1,130,512]{2,1,0:T(8,128)(2,1)S(1)}, u32[]{:S(2)}, u32[]{:S(2)}) collective-permute-start(bf16[1,130,512]{2,1,0:T(8,128)(2,1)S(1)} %get-tuple-element.149), channel_id=1, source_target_pairs={{0,16},{16,32},{32,48},{1,17},{17,33},{33,49},{2,18},{18,34},{34,5... | collective-permute-start | bytes 399368 | tf_op jit(solution)/shard_map/ppermute | solution.py:21
  356.4 1.9 collective-permute-start.3
  358.4 2.6 broadcast_in_dim.12
  360.9 5.3 %select_n.20 = f32[16,128,512]{2,1,0:T(8,128)} reshape(f32[16,256,256]{2,1,0:T(8,128)} %broadcast_in_dim.12) | data formatting | bytes 8388608 | tf_op jit(solution)/shard_map/jit(_where)/select_n | solution.py:205
  366.7 0.7 reduce.3
  367.6 2.2 pad_maximum_fusion
  369.8 48.9 %conditional.4 = (f32[16,128,512]{2,1,0:T(8,128)}) conditional(s32[]{:T(128)} %convert_element_type.59, (bf16[18,130,512]{2,1,0:T(8,128)(2,1)}, bf16[2,3,3,512,512]{4,3,2,1,0:T(8,128)(2,1)}, bf16[16,130,512]{2,1,0:T(8,128)(2,1)S(1)}, bf16[16,128,512]{2,1,0:T(8,128)(2,1)S(1)}) %tuple.85, (bf16[18,130,512]{2,1,0:T(8,128)(2,1)}, ...), branch_computations={%region_0.0_spmd, %region_1.0_spmd} | conditional | flops 9672065024 | bytes 174530688 | solution.py:211
  369.8 1.1 fusion.44
  371.0 2.6 slice_bitcast_fusion
  373.6 1.2 fusion.2
  374.9 1.3 fusion.3
  376.1 1.3 fusion.4
  377.4 11.0 %fusion.43 = (bf16[16,128,512]{2,1,0:T(8,128)(2,1)}, bf16[16,128,512]{2,1,0:T(8,128)(2,1)}, bf16[16,128,512]{2,1,0:T(8,128)(2,1)S(1)}, bf16[16,128,512]{2,1,0:T(...) fusion(bf16[18,130,512]{2,1,0:T(8,128)(2,1)} %get-tuple-element.71), kind=kLoop, calls=%fused_computation.134 | loop fusion | bytes 25165824 | tf_op jit(solution)/shard_map/cond/branch_0_fun/slice | solution.py:63
  388.4 4.9 fusion
  393.4 3.2 fusion.1
  396.6 3.3 fusion.5
  399.9 3.4 fusion.6
  403.3 3.3 fusion.7
  406.6 12.0 %add_add_fusion = f32[2048,512]{1,0:T(8,128)} fusion(f32[2048,512]{1,0:T(8,128)} %fusion, f32[2048,512]{1,0:T(8,128)} %fusion.1, f32[2048,512]{1,0:T(8,128)S(1)} %fusion.2, f32[2048,512]{1,0:T(8,128)S(1)} %fusion.3, f32[2048,512]{1,0:T(8,128)S(1)} %fusion.4, f32[2048,512]{1,0:T(8,128)} %fusion.5, f32[2048,512]{1,0:T(8,128)} %fusion.7, ...), kind=kOutput, calls=%fused_computation.3 | convolution fusion | flops 1082130432 | bytes 40370176 | tf_op jit(solution)/shard_map/cond/branch_0_fun/dot_general | solution.py:66
  418.8 26.1 %conditional.6 = (f32[16,128,512]{2,1,0:T(8,128)}) conditional(s32[]{:T(128)} %convert_element_type.59, (s32[128]{0:T(128)S(1)}, bf16[128,128,256]{2,1,0:T(8,128)(2,1)}, bf16[256,512]{1,0:T(8,128)(2,1)S(1)}) %tuple.87, (s32[128]{0:T(128)S(1)}, bf16[128,128,256]{2,1,0:T(8,128)(2,1)}) %tuple.34), branch_computations={%region_7.8_spmd, %region_8.9_spmd} | conditional | flops 671614976 | bytes 46138120 | solution.py:219
  424.9 12.4 %copy.49 = bf16[16,8,128,256]{3,1,2,0:T(8,128)(2,1)} copy(bf16[16,8,128,256]{3,2,1,0:T(8,128)(2,1)} %bitcast.110) | data formatting | bytes 16777216 | tf_op jit(solution)/shard_map/cond
  437.3 4.6 convolution_convert_fusion
  442.1 2.6 fusion.9
  444.9 6.7 %fusion.28 = (bf16[16,128,512]{2,1,0:T(8,128)(2,1)S(1)}, bf16[16,128,512]{2,1,0:T(8,128)(2,1)}) fusion(f32[16,128,512]{2,1,0:T(8,128)} %select_n.20, f32[16,128,512]{2,1,0:T(8,128)} %get-tuple-element.160, f32[16,128,512]{2,1,0:T(8,128)} %get-tuple-element.158, bf16[1,16,128,512]{3,2,1,0:T(8,128)(2,1)S(1)} %copy-done.6), kind=kLoop, calls=%fused_computation.105 | loop fusion | flops 11534336 | bytes 18874368 | tf_op jit(solution)/shard_map/convert_element_type | solution.py:209
  451.8 3.8 collective-permute-start.7
  455.7 1.6 collective-permute-done.6
  457.3 1.3 pad_maximum_fusion.3
  458.6 3.9 collective-permute-start.8
  462.5 1.9 collective-permute-start.9
  464.4 1.1 collective-permute-done.8
  465.5 3.9 collective-permute-done.9
  469.4 2.2 pad_maximum_fusion.1
  471.7 46.5 %conditional.7 = (f32[16,128,512]{2,1,0:T(8,128)}) conditional(s32[]{:T(128)} %convert_element_type.59, (bf16[18,130,512]{2,1,0:T(8,128)(2,1)}, bf16[2,3,3,512,512]{4,3,2,1,0:T(8,128)(2,1)S(1)}, bf16[16,130,512]{2,1,0:T(8,128)(2,1)S(1)}, bf16[16,128,512]{2,1,0:T(8,128)(2,1)S(1)}) %tuple.86, (bf16[18,130,512]{2,1,0:T(8,128)(2,1)}, ...), branch_computations={%region_9.10_spmd, %region_10.11_spmd} | conditional | flops 9672065024 | bytes 174530688 | solution.py:211
  471.7 1.2 fusion.47
  473.2 1.3 fusion.18
  474.5 1.3 fusion.19
  475.7 1.3 fusion.20
  477.0 10.8 %fusion.46 = (bf16[16,128,512]{2,1,0:T(8,128)(2,1)}, bf16[16,128,512]{2,1,0:T(8,128)(2,1)}, bf16[16,128,512]{2,1,0:T(8,128)(2,1)S(1)}, bf16[16,128,512]{2,1,0:T(...) fusion(bf16[18,130,512]{2,1,0:T(8,128)(2,1)} %get-tuple-element.88), kind=kLoop, calls=%fused_computation.137 | loop fusion | bytes 25165824 | tf_op jit(solution)/shard_map/cond/branch_0_fun/slice | solution.py:63
  487.9 4.9 fusion.16
  492.7 3.4 fusion.17
  496.1 3.2 fusion.21
  499.3 3.4 fusion.22
  502.7 3.3 fusion.23
  506.0 12.0 %add_add_fusion.1 = f32[2048,512]{1,0:T(8,128)} fusion(f32[2048,512]{1,0:T(8,128)} %fusion.16, f32[2048,512]{1,0:T(8,128)} %fusion.17, f32[2048,512]{1,0:T(8,128)S(1)} %fusion.18, f32[2048,512]{1,0:T(8,128)S(1)} %fusion.19, f32[2048,512]{1,0:T(8,128)S(1)} %fusion.20, f32[2048,512]{1,0:T(8,128)} %fusion.21, f32[2048,512]{1,0:T(8,128)} %fusion.23, ...), kind=kOutput, calls=%fused_computation.52 | convolution fusion | flops 1082130432 | bytes 40370176 | tf_op jit(solution)/shard_map/cond/branch_0_fun/dot_general | solution.py:66
  518.2 6.8 %fusion.38 = bf16[1,16,128,512]{3,2,1,0:T(8,128)(2,1)} fusion(f32[16,128,512]{2,1,0:T(8,128)} %select_n.20, f32[16,128,512]{2,1,0:T(8,128)} %get-tuple-element.161, bf16[16,128,512]{2,1,0:T(8,128)(2,1)} %get-tuple-element.112), kind=kLoop, calls=%fused_computation.120 | loop fusion | flops 4194304 | bytes 12582912 | tf_op jit(solution)/shard_map/broadcast_in_dim | solution.py:221
  (51 shorter events, 2.5 us)
Async XLA Ops:
  0.0 7.9 %copy-start = (bf16[1,1,1,64,128,128]{5,4,3,2,1,0:T(8,128)(2,1)S(1)}, bf16[1,1,1,64,128,128]{5,4,3,2,1,0:T(8,128)(2,1)}, u32[]{:S(2)}) copy-start(bf16[1,1,1,64,128,128]{5,4,3,2,1,0:T(8,128)(2,1)} %param.18) | copy-start | bytes 6291460
  37.2 206.4 %collective-permute-start.5 = (bf16[128,128,256]{2,1,0:T(8,128)(2,1)}, bf16[128,128,256]{2,1,0:T(8,128)(2,1)}, u32[]{:S(2)}, u32[]{:S(2)}) collective-permute-start(bf16[128,128,256]{2,1,0:T(8,128)(2,1)} %bitcast.291), channel_id=1, source_target_pairs={{0,64},{64,0},{1,65},{65,1},{2,66},{66,2},{3,67},{67,3},{4,68},{68... | collective-permute-start | bytes 25165832 | tf_op jit(solution)/shard_map/ppermute | solution.py:32
  47.4 180.7 %collective-permute-start.4 = (s32[128]{0:T(128)S(1)}, s32[128]{0:T(128)S(1)}, u32[]{:S(2)}, u32[]{:S(2)}) collective-permute-start(s32[128]{0:T(128)S(1)} %broadcast_add_fusion), channel_id=1, source_target_pairs={{0,64},{64,0},{1,65},{65,1},{2,66},{66,2},{3,67},{67,3},{4,68},{68... | collective-permute-start | bytes 1544 | tf_op jit(solution)/shard_map/ppermute | solution.py:32
  243.6 175.2 %all-to-all-start.1 = ((bf16[128,128,256]{2,1,0:T(8,128)(2,1)}), bf16[128,128,256]{2,1,0:T(8,128)(2,1)}, u32[]{:S(2)}, u32[]{:S(2)}) async-start(bf16[128,128,256]{2,1,0:T(8,128)(2,1)} %collective-permute-done.5), calls=%async_computation.1 | async-start | bytes 16777216 | tf_op jit(solution)/shard_map/all_to_all | solution.py:99
  253.6 104.8 %copy-start.16 = (s32[16,256]{1,0:T(8,128)S(1)}, s32[16,256]{1,0:T(8,128)}, u32[]{:S(2)}) copy-start(s32[16,256]{1,0:T(8,128)} %param.19) | copy-start | bytes 49156
  253.6 94.7 %collective-permute-start = (bf16[16,1,512]{2,1,0:T(2,128)(2,1)S(1)}, bf16[16,1,512]{2,1,0:T(2,128)(2,1)S(1)}, u32[]{:S(2)}, u32[]{:S(2)}) collective-permute-start(bf16[16,1,512]{2,1,0:T(2,128)(2,1)S(1)} %get-tuple-element.153), channel_id=1, source_target_pairs={{0,1},{1,2},{2,3},{3,4},{4,5},{5,6},{6,7},{7,8},{8,9},{9,10},{10,1... | collective-permute-start | bytes 49160 | tf_op jit(solution)/shard_map/ppermute | solution.py:21
  253.8 94.5 %collective-permute-start.1 = (bf16[16,1,512]{2,1,0:T(2,128)(2,1)S(1)}, bf16[16,1,512]{2,1,0:T(2,128)(2,1)S(1)}, u32[]{:S(2)}, u32[]{:S(2)}) collective-permute-start(bf16[16,1,512]{2,1,0:T(2,128)(2,1)S(1)} %get-tuple-element.154), channel_id=1, source_target_pairs={{1,0},{2,1},{3,2},{4,3},{5,4},{6,5},{7,6},{8,7},{9,8},{10,9},{11,1... | collective-permute-start | bytes 49160 | tf_op jit(solution)/shard_map/ppermute | solution.py:24
  349.5 1.3 copy-start.2
  350.9 16.7 %collective-permute-start.2 = (bf16[1,130,512]{2,1,0:T(8,128)(2,1)S(1)}, bf16[1,130,512]{2,1,0:T(8,128)(2,1)S(1)}, u32[]{:S(2)}, u32[]{:S(2)}) collective-permute-start(bf16[1,130,512]{2,1,0:T(8,128)(2,1)S(1)} %get-tuple-element.149), channel_id=1, source_target_pairs={{0,16},{16,32},{32,48},{1,17},{17,33},{33,49},{2,18},{18,34},{34,5... | collective-permute-start | bytes 399368 | tf_op jit(solution)/shard_map/ppermute | solution.py:21
  356.4 11.2 %collective-permute-start.3 = (bf16[1,130,512]{2,1,0:T(8,128)(2,1)S(1)}, bf16[1,130,512]{2,1,0:T(8,128)(2,1)S(1)}, u32[]{:S(2)}, u32[]{:S(2)}) collective-permute-start(bf16[1,130,512]{2,1,0:T(8,128)(2,1)S(1)} %get-tuple-element.150), channel_id=1, source_target_pairs={{16,0},{32,16},{48,32},{17,1},{33,17},{49,33},{18,2},{34,18},{50,3... | collective-permute-start | bytes 399368 | tf_op jit(solution)/shard_map/ppermute | solution.py:24
  367.6 2.3 copy-start.3
  369.8 48.9 %copy-start.15 = (bf16[256,512]{1,0:T(8,128)(2,1)S(1)}, bf16[256,512]{1,0:T(8,128)(2,1)}, u32[]{:S(2)}) copy-start(bf16[256,512]{1,0:T(8,128)(2,1)} %param.23) | copy-start | bytes 786436
  373.6 29.7 %copy-start.4 = (bf16[3,3,512,512]{3,2,1,0:T(8,128)(2,1)}, bf16[3,3,512,512]{3,2,1,0:T(8,128)(2,1)S(1)}, u32[]{:S(2)}) copy-start(bf16[3,3,512,512]{3,2,1,0:T(8,128)(2,1)S(1)} %slice_bitcast_fusion) | copy-start | bytes 14155780 | tf_op jit(solution)/shard_map/cond
  418.7 26.2 %copy-start.6 = (bf16[1,16,128,512]{3,2,1,0:T(8,128)(2,1)S(1)}, bf16[1,16,128,512]{3,2,1,0:T(8,128)(2,1)}, u32[]{:S(2)}) copy-start(bf16[1,16,128,512]{3,2,1,0:T(8,128)(2,1)} %param.16) | copy-start | bytes 6291460
  444.9 26.7 %slice-start = ((s8[9437184]{0:T(1024)(128)(4,1)}), s8[4194304]{0:T(1024)(128)(4,1)S(1)}, s32[]{:S(2)}) async-start(s8[9437184]{0:T(1024)(128)(4,1)} %bitcast.287), calls=%async_computation.2 | async-start | bytes 8388608
  444.9 26.7 %slice-start.1 = ((s8[9437184]{0:T(1024)(128)(4,1)}), s8[4194304]{0:T(1024)(128)(4,1)S(1)}, s32[]{:S(2)}) async-start(s8[9437184]{0:T(1024)(128)(4,1)} %bitcast.287), calls=%async_computation.3 | async-start | bytes 8388608
  451.7 5.5 %collective-permute-start.6 = (bf16[16,1,512]{2,1,0:T(2,128)(2,1)S(1)}, bf16[16,1,512]{2,1,0:T(2,128)(2,1)S(1)}, u32[]{:S(2)}, u32[]{:S(2)}) collective-permute-start(bf16[16,1,512]{2,1,0:T(2,128)(2,1)S(1)} %get-tuple-element.151), channel_id=1, source_target_pairs={{0,1},{1,2},{2,3},{3,4},{4,5},{5,6},{6,7},{7,8},{8,9},{9,10},{10,1... | collective-permute-start | bytes 49160 | tf_op jit(solution)/shard_map/ppermute | solution.py:21
  451.8 19.8 %slice-start.2 = ((s8[9437184]{0:T(1024)(128)(4,1)}), s8[1048576]{0:T(1024)(128)(4,1)S(1)}, s32[]{:S(2)}) async-start(s8[9437184]{0:T(1024)(128)(4,1)} %bitcast.287), calls=%async_computation.4 | async-start | bytes 2097152
  451.8 5.4 %collective-permute-start.7 = (bf16[16,1,512]{2,1,0:T(2,128)(2,1)S(1)}, bf16[16,1,512]{2,1,0:T(2,128)(2,1)S(1)}, u32[]{:S(2)}, u32[]{:S(2)}) collective-permute-start(bf16[16,1,512]{2,1,0:T(2,128)(2,1)S(1)} %get-tuple-element.152), channel_id=1, source_target_pairs={{1,0},{2,1},{3,2},{4,3},{5,4},{6,5},{7,6},{8,7},{9,8},{10,9},{11,1... | collective-permute-start | bytes 49160 | tf_op jit(solution)/shard_map/ppermute | solution.py:24
  458.6 6.9 %collective-permute-start.8 = (bf16[1,130,512]{2,1,0:T(8,128)(2,1)S(1)}, bf16[1,130,512]{2,1,0:T(8,128)(2,1)S(1)}, u32[]{:S(2)}, u32[]{:S(2)}) collective-permute-start(bf16[1,130,512]{2,1,0:T(8,128)(2,1)S(1)} %get-tuple-element.147), channel_id=1, source_target_pairs={{0,16},{16,32},{32,48},{1,17},{17,33},{33,49},{2,18},{18,34},{34,5... | collective-permute-start | bytes 399368 | tf_op jit(solution)/shard_map/ppermute | solution.py:21
  462.5 6.9 %collective-permute-start.9 = (bf16[1,130,512]{2,1,0:T(8,128)(2,1)S(1)}, bf16[1,130,512]{2,1,0:T(8,128)(2,1)S(1)}, u32[]{:S(2)}, u32[]{:S(2)}) collective-permute-start(bf16[1,130,512]{2,1,0:T(8,128)(2,1)S(1)} %get-tuple-element.148), channel_id=1, source_target_pairs={{16,0},{32,16},{48,32},{17,1},{33,17},{49,33},{18,2},{34,18},{50,3... | collective-permute-start | bytes 399368 | tf_op jit(solution)/shard_map/ppermute | solution.py:24
  473.2 29.6 %copy-start.5 = (bf16[3,3,512,512]{3,2,1,0:T(8,128)(2,1)}, bf16[3,3,512,512]{3,2,1,0:T(8,128)(2,1)S(1)}, u32[]{:S(2)}) copy-start(bf16[3,3,512,512]{3,2,1,0:T(8,128)(2,1)S(1)} %slice_bitcast_fusion.38) | copy-start | bytes 14155780 | tf_op jit(solution)/shard_map/cond
  518.2 6.8 %copy-start.1 = (bf16[1,1,1,64,128,128]{5,4,3,2,1,0:T(8,128)(2,1)S(1)}, bf16[1,1,1,64,128,128]{5,4,3,2,1,0:T(8,128)(2,1)}, u32[]{:S(2)}) copy-start(bf16[1,1,1,64,128,128]{5,4,3,2,1,0:T(8,128)(2,1)} %param.18) | copy-start | bytes 6291460
where the time goes:
time: 535 us; the launch traced here: 525 us
  waiting for transfers between devices  278 us (52%)
  matrix products  90.7 us (17%)
  local copies, waits for them, and re-layouts  68.8 us (13%)
  starting transfers between devices  38.4 us (7%)
  other arithmetic  26.6 us (5%)
  blocking collectives  15.4 us (3%)
  loops' own time  6.74 us (1%)
    ppermute x2, waiting for transfers between devices, partner(): return lax.ppermute(value, axis, pairs)  181 us
    ppermute x4, waiting for transfers between devices, extended(): lax.ppermute(lax.slice_in_dim(block, block.shape[dim] - width, None, axis...  93.4 us
    dot_general x18, matrix products, shifted_conv(): jnp.dot(window, kernel[shift_row, shift_col], preferred_element_type=jnp....  67.9 us
    slice x4, local copies, waits for them, and re-layouts, shifted_conv(): padded[shift_row:shift_row + patch_span_down, shift_col:shift_col + patch...  24.2 us
    unnamed x22, local copies, waits for them, and re-layouts  17.3 us
    all_to_all x1, blocking collectives, within(): lax.all_to_all(labels, ('lat', 'lon'), split_axis=0, concat_axis=0, tiled...  15.4 us
    cond x5, local copies, waits for them, and re-layouts  12.4 us
    ppermute x4, starting transfers between devices, extended(): lax.ppermute(lax.slice_in_dim(block, 0, width, axis=dim), axis, backward)  11.4 us
  transfers between devices with their start and end apart: 11, of which 5 were waited for; matrix products, arithmetic and copies ran while one was open for 12% of the time, Pallas kernels for 0%

commit v1 on v0

v1 whole, which is shorter than its diff:
```python
from functools import partial

import jax
import jax.numpy as jnp
from jax import lax
from jax.experimental import pallas as pl
from jax.experimental.pallas import tpu as pltpu
from jax.sharding import PartitionSpec as P

LAYERS = 2
ROWS = 16
COLS = 128
WIDE = 512
HALF = 256
BLOCK = 128
ENTRIES = 64
TILES = 64
CHUNKS = 4
PIECE = BLOCK // CHUNKS
SLOT_TOTAL = 2 * TILES
MESH = pl.DeviceIdType.MESH
F32 = jnp.float32
BF16 = jnp.bfloat16


def dot(a, b):
    return jnp.dot(a, b, preferred_element_type=F32)


def place_entries(lists, counts, places, labels_ref):
    def clear(i, _):
        counts[i] = 0
        labels_ref[0, 2 * i] = -1
        labels_ref[0, 2 * i + 1] = -1
        return 0

    lax.fori_loop(0, TILES, clear, 0)

    def place(e, _):
        owner = lists[0, e]
        rank = counts[owner]
        counts[owner] = rank + 1
        slot = 2 * (owner ^ 8) + rank
        places[e] = slot
        labels_ref[0, slot] = lists[2, e]
        return 0

    lax.fori_loop(0, ENTRIES, place, 0)


def write_payloads(lists, places, factors, blocks, out_ref):
    def one(e, _):
        value = dot(factors[e], blocks[lists[1, e]])
        out_ref[0, places[e]] = value.astype(BF16)
        return 0

    lax.fori_loop(0, ENTRIES, one, 0, unroll=8)


def air_payloads(lists, state, factors, projection, out_ref, labels_ref, blocks, counts, places):
    @pl.when(pl.program_id(0) == 0)
    def _():
        place_entries(lists, counts, places, labels_ref)
        for row in range(ROWS):
            flux = dot(state[row], projection[...]).astype(BF16)
            band, sub = row // 8, row % 8
            blocks[8 * band : 8 * band + 8, 16 * sub : 16 * sub + 16, :] = flux.reshape(8, 16, HALF)

    write_payloads(lists, places, factors, blocks, out_ref)


def interleave_matrix():
    cell = lax.broadcasted_iota(jnp.int32, (BLOCK, BLOCK), 0)
    place = lax.broadcasted_iota(jnp.int32, (BLOCK, BLOCK), 1)
    wanted = (cell % 2) * 64 + (cell // 16) * 8 + (cell % 16) // 2
    return (wanted == place).astype(F32).astype(BF16)


def sea_payloads(lists, state, factors, water, out_ref, labels_ref, halves, blocks, counts, places):
    @pl.when(pl.program_id(0) == 0)
    def _():
        place_entries(lists, counts, places, labels_ref)
        for row in range(ROWS):
            band, sub = row // 8, row % 8
            for side in range(2):
                surface = state[row, :, side * HALF : (side + 1) * HALF].astype(F32)
                surface = surface * water[row, :, side : side + 1]
                start = 64 * side + 8 * sub
                halves[16 * band : 16 * band + 16, start : start + 8, :] = surface.reshape(16, 8, HALF)
        order = interleave_matrix()

        def one(b, _):
            blocks[b] = dot(order, halves[b].astype(BF16)).astype(BF16)
            return 0

        lax.fori_loop(0, 32, one, 0, unroll=4)

    write_payloads(lists, places, factors, blocks, out_ref)


def payload_call(kernel, block_total, extra, lists, state, factors, side):
    whole = lambda shape: pl.BlockSpec(shape, lambda c, *_: (0,) * len(shape))
    return pl.pallas_call(
        kernel,
        out_shape=(
            jax.ShapeDtypeStruct((CHUNKS, SLOT_TOTAL, PIECE, HALF), BF16),
            jax.ShapeDtypeStruct((1, SLOT_TOTAL), jnp.int32),
        ),
        grid_spec=pltpu.PrefetchScalarGridSpec(
            num_scalar_prefetch=1,
            grid=(CHUNKS,),
            in_specs=[
                whole(state.shape),
                pl.BlockSpec((ENTRIES, PIECE, BLOCK), lambda c, *_: (0, c, 0)),
                whole(side.shape),
            ],
            out_specs=(
                pl.BlockSpec((1, SLOT_TOTAL, PIECE, HALF), lambda c, *_: (c, 0, 0, 0)),
                pl.BlockSpec(memory_space=pltpu.SMEM),
            ),
            scratch_shapes=extra
            + [
                pltpu.VMEM((block_total, BLOCK, HALF), BF16),
                pltpu.SMEM((TILES,), jnp.int32),
                pltpu.SMEM((ENTRIES,), jnp.int32),
            ],
        ),
        compiler_params=pltpu.CompilerParams(vmem_limit_bytes=40 << 20),
    )(lists, state, factors, side)


def sort_slots(labels_ref, me, orders):
    labels = labels_ref[...].reshape(TILES, SLOT_TOTAL)
    lane = lax.broadcasted_iota(jnp.int32, (TILES, SLOT_TOTAL), 1)
    first = jnp.sum(jnp.where(lane == 2 * me, labels, 0), axis=1, keepdims=True)
    second = jnp.sum(jnp.where(lane == 2 * me + 1, labels, 0), axis=1, keepdims=True)
    column = jnp.concatenate([first, second], axis=0)
    down = lax.broadcasted_iota(jnp.int32, (SLOT_TOTAL, SLOT_TOTAL), 0)
    across = lax.broadcasted_iota(jnp.int32, (SLOT_TOTAL, SLOT_TOTAL), 1)
    keys = jnp.broadcast_to(column, (SLOT_TOTAL, SLOT_TOTAL))
    row = jnp.sum(jnp.where(down == across, keys, 0), axis=0, keepdims=True)
    other = jnp.broadcast_to(row, (SLOT_TOTAL, SLOT_TOTAL))
    ahead = (other < keys) | ((other == keys) & (across < down))
    rank = jnp.sum(ahead.astype(jnp.int32), axis=1, keepdims=True)
    hit = rank == across
    slot = 2 * (down % TILES) + down // TILES
    order = jnp.sum(jnp.where(hit, slot, 0), axis=0, keepdims=True)
    sorted_keys = jnp.sum(jnp.where(hit, keys, 0), axis=0, keepdims=True)
    previous = jnp.sum(jnp.where(rank + 1 == across, keys, 0), axis=0, keepdims=True)
    lanes = lax.broadcasted_iota(jnp.int32, (1, SLOT_TOTAL), 1)
    opens = ((sorted_keys != previous) | (lanes == 0)).astype(jnp.int32)
    count = jnp.sum((keys == across).astype(jnp.int32), axis=0, keepdims=True)
    last = jnp.sum((keys <= across).astype(jnp.int32), axis=0, keepdims=True) - 1
    last = jnp.maximum(last, 0)
    orders[...] = jnp.concatenate([order, opens, last, count, order, opens, last, count], axis=0)


def exchange(payload, labels, out_ref, recv_0, recv_1, recv_2, recv_3, marks, orders, table, sums, leaving, arriving, sent, landed, own, mark_sem, local_sem, over_sent, over_landed):
    recv = [recv_0, recv_1, recv_2, recv_3]
    grp, lat, lon = lax.axis_index("grp"), lax.axis_index("lat"), lax.axis_index("lon")
    me = lat * 16 + lon
    high, x, core = lon // 8, (lon // 2) % 4, lon % 2
    facing = (1 - grp, lat, (lon + 8) % 16)

    def target(k):
        z = (lat + k) % 4
        y = (high + k // 16 + k // 2) % 2
        c = (core + k // 32 + k) % 2
        return z, y * 8 + ((x + k // 4 + k) % 4) * 2 + c

    barrier = pltpu.get_barrier_semaphore()

    def greet(k, _):
        z, j = target(k)
        pl.semaphore_signal(barrier, inc=1, device_id=(grp, z, j), device_id_type=MESH)
        return 0

    lax.fori_loop(1, TILES, greet, 0)
    pl.semaphore_signal(barrier, inc=1, device_id=facing, device_id_type=MESH)
    pl.semaphore_wait(barrier, TILES)

    def send_label(k, _):
        z, j = target(k)
        pltpu.make_async_remote_copy(
            labels, marks.at[me], mark_sem.at[0], mark_sem.at[1], device_id=(grp, z, j), device_id_type=MESH
        ).start()
        return 0

    lax.fori_loop(1, TILES, send_label, 0)
    mine = pltpu.make_async_copy(labels, marks.at[me], local_sem.at[0])
    mine.start()

    for chunk in range(CHUNKS):

        def send(k, _):
            z, j = target(k)
            pltpu.make_async_remote_copy(
                payload.at[chunk, pl.ds(2 * (z * 16 + j), 2)],
                recv[chunk].at[pl.ds(2 * me, 2)],
                sent.at[chunk],
                landed.at[chunk],
                device_id=(grp, z, j),
                device_id_type=MESH,
            ).start()
            return 0

        lax.fori_loop(1, TILES, send, 0)
        pltpu.make_async_copy(
            payload.at[chunk, pl.ds(2 * me, 2)], recv[chunk].at[pl.ds(2 * me, 2)], own.at[chunk]
        ).start()

    mine.wait()
    others = pltpu.make_async_remote_copy(
        marks.at[pl.ds(0, TILES - 1)],
        marks.at[pl.ds(0, TILES - 1)],
        mark_sem.at[0],
        mark_sem.at[1],
        device_id=facing,
        device_id_type=MESH,
    )
    others.wait_recv()
    others.wait_send()
    sort_slots(marks, me, orders)
    move = pltpu.make_async_copy(orders, table, local_sem.at[1])
    move.start()
    move.wait()

    def crossing(chunk, part):
        blocks = pl.ds(16 * part, 16)
        return pltpu.make_async_remote_copy(
            leaving.at[chunk, blocks],
            arriving.at[chunk, blocks],
            over_sent.at[chunk, part],
            over_landed.at[chunk, part],
            device_id=facing,
            device_id_type=MESH,
        )

    for chunk in range(CHUNKS):
        pltpu.make_async_copy(
            payload.at[chunk, pl.ds(2 * me, 2)], recv[chunk].at[pl.ds(2 * me, 2)], own.at[chunk]
        ).wait()
        rest = pltpu.make_async_remote_copy(
            payload.at[chunk, pl.ds(0, SLOT_TOTAL - 2)],
            recv[chunk].at[pl.ds(0, SLOT_TOTAL - 2)],
            sent.at[chunk],
            landed.at[chunk],
            device_id=facing,
            device_id_type=MESH,
        )
        rest.wait_recv()
        rest.wait_send()

        def accumulate(p, total):
            value = recv[chunk][table[0, p]].astype(F32)
            total = jnp.where(table[1, p] == 1, 0.0, total) + value
            sums[p] = total
            return total

        lax.fori_loop(0, SLOT_TOTAL, accumulate, jnp.zeros((PIECE, HALF), F32), unroll=8)

        def settle(b, _):
            value = jnp.where(table[3, b] > 0, sums[table[2, b]], 0.0)
            leaving[chunk, b] = value.astype(BF16)
            return 0

        lax.fori_loop(0, 32, settle, 0, unroll=4)
        crossing(chunk, 0).start()

        @pl.when(grp == 0)
        def _():
            crossing(chunk, 1).start()

    for chunk in range(CHUNKS):
        crossing(chunk, 0).wait()

        @pl.when(grp == 0)
        def _():
            crossing(chunk, 1).wait_send()

        @pl.when(grp == 1)
        def _():
            crossing(chunk, 1).wait_recv()

    out = pltpu.make_async_copy(arriving.at[:, pl.ds(0, 16)], out_ref.at[:, pl.ds(0, 16)], local_sem.at[2])
    out.start()

    @pl.when(grp == 1)
    def _():
        rest = pltpu.make_async_copy(
            arriving.at[:, pl.ds(16, 16)], out_ref.at[:, pl.ds(16, 16)], local_sem.at[3]
        )
        rest.start()
        rest.wait()

    out.wait()


def exchange_call(payload, labels):
    dma = pltpu.SemaphoreType.DMA
    return pl.pallas_call(
        exchange,
        out_shape=jax.ShapeDtypeStruct((CHUNKS, 32, PIECE, HALF), BF16),
        in_specs=[pl.BlockSpec(memory_space=pl.ANY), pl.BlockSpec(memory_space=pltpu.VMEM)],
        out_specs=pl.BlockSpec(memory_space=pl.ANY),
        scratch_shapes=[pltpu.VMEM((SLOT_TOTAL, PIECE, HALF), BF16)] * CHUNKS
        + [
            pltpu.VMEM((TILES, 1, SLOT_TOTAL), jnp.int32),
            pltpu.VMEM((8, SLOT_TOTAL), jnp.int32),
            pltpu.SMEM((8, SLOT_TOTAL), jnp.int32),
            pltpu.VMEM((SLOT_TOTAL, PIECE, HALF), F32),
            pltpu.VMEM((CHUNKS, 32, PIECE, HALF), BF16),
            pltpu.VMEM((CHUNKS, 32, PIECE, HALF), BF16),
            dma((CHUNKS,)),
            dma((CHUNKS,)),
            dma((CHUNKS,)),
            dma((2,)),
            dma((4,)),
            dma((CHUNKS, 2)),
            dma((CHUNKS, 2)),
        ],
        compiler_params=pltpu.CompilerParams(
            collective_id=0, has_side_effects=True, vmem_limit_bytes=48 << 20
        ),
    )(payload, labels)


def silu(value):
    return value / (1.0 + jnp.exp(-value))


def rows_with_rims(sides, rims, lat):
    above = rims[0].astype(F32)[15:16] * jnp.where(lat == 0, 0.0, 1.0)
    below = rims[2].astype(F32)[0:1] * jnp.where(lat == 3, 0.0, 1.0)
    sides[0:1, :] = above
    sides[1:17, :] = rims[1].astype(F32)
    sides[17:18, :] = below


def layer_kernel(layer, forced, state, force, coupling, water, air_kernels, sea_kernels, out_ref, padded, edges, rims, sides, ends, air, sea, fetch, sent, landed):
    grp, lat, lon = lax.axis_index("grp"), lax.axis_index("lat"), lax.axis_index("lon")
    west, east = (lon + 15) % 16, (lon + 1) % 16
    north, south = (lat + 3) % 4, (lat + 1) % 4

    get_air = pltpu.make_async_copy(air_kernels.at[layer], air, fetch)
    get_sea = pltpu.make_async_copy(sea_kernels.at[layer], sea, fetch)

    @pl.when(grp == 0)
    def _():
        get_air.start()

    @pl.when(grp == 1)
    def _():
        get_sea.start()

    barrier = pltpu.get_barrier_semaphore()
    near = [(north, lon), (south, lon)] + [(z, j) for j in (west, east) for z in (north, lat, south)]
    for z, j in near:
        pl.semaphore_signal(barrier, inc=1, device_id=(grp, z, j), device_id_type=MESH)

    def activate(row, _):
        padded[row + 1] = silu(state[row].astype(F32)).astype(BF16)
        return 0

    lax.fori_loop(0, ROWS, activate, 0, unroll=2)
    for side, first in ((0, 0), (1, COLS - 16)):
        group = padded[1:17, first : first + 16, :].astype(F32)
        edges[side] = group[:, 15 * side, :].astype(BF16)

    pl.semaphore_wait(barrier, 8)

    def push(index, source, target, z, j):
        copy = pltpu.make_async_remote_copy(
            source, target, sent.at[index], landed.at[index], device_id=(grp, z, j), device_id_type=MESH
        )
        copy.start()
        return copy

    copies = [
        push(0, padded.at[1], padded.at[17], north, lon),
        push(1, padded.at[16], padded.at[0], south, lon),
    ]
    for side, j in ((0, west), (1, east)):
        for index, z, place in ((0, north, 2), (1, lat, 1), (2, south, 0)):
            copies.append(push(2 + 3 * side + index, edges.at[side], rims.at[1 - side, place], z, j))
    for copy in copies:
        copy.wait()

    @pl.when(lat == 0)
    def _():
        padded[0] = jnp.zeros((COLS, WIDE), BF16)

    @pl.when(lat == 3)
    def _():
        padded[17] = jnp.zeros((COLS, WIDE), BF16)

    for side in range(2):
        rows_with_rims(sides.at[side], rims.at[side], lat)
    column = lax.broadcasted_iota(jnp.int32, (COLS, 1), 0)

    def moved(value, edge, shift):
        rolled = pltpu.roll(value, shift % COLS, 0)
        return jnp.where(column == (0 if shift == 1 else COLS - 1), edge, rolled)

    @pl.when(grp == 0)
    def _():
        get_air.wait()
        for side, tap in ((0, 0), (1, 2)):
            ends[side] = sum(dot(sides[side, r : r + 16, :].astype(BF16), air[r, tap]) for r in range(3))

        def some_rows(step, _):
            first = 4 * step
            parts = []
            for tap in range(3):
                total = None
                for r in range(3):
                    window = padded[pl.ds(first + r, 4)].reshape(4 * COLS, WIDE)
                    term = dot(window, air[r, tap])
                    total = term if total is None else total + term
                parts.append(total)
            for i in range(4):
                row = first + i
                low = slice(i * COLS, (i + 1) * COLS)
                value = state[row].astype(F32) + parts[1][low]
                value = value + moved(parts[0][low], ends[0, pl.ds(row, 1), :], 1)
                value = value + moved(parts[2][low], ends[1, pl.ds(row, 1), :], -1)
                if forced:
                    given = force[i // 2 + 2 * (step % 2), pl.ds(8 * (step // 2), 8), 16 * (i % 2) : 16 * (i % 2) + 16, :]
                    value = value + dot(given.reshape(COLS, HALF), coupling[...])
                out_ref[row] = value.astype(BF16)
            return 0

        lax.fori_loop(0, 4, some_rows, 0)

    @pl.when(grp == 1)
    def _():
        get_sea.wait()
        ends[0, :, 0:HALF] = sum(dot(sides[0, r : r + 16, HALF:].astype(BF16), sea[r, 0]) for r in range(3))
        ends[1, :, 0:HALF] = sum(dot(sides[1, r : r + 16, :HALF].astype(BF16), sea[r, 2]) for r in range(3))
        cell = lax.broadcasted_iota(jnp.int32, (COLS, 2 * COLS), 1)
        pair = lax.broadcasted_iota(jnp.int32, (COLS, 2 * COLS), 0)

        def some_rows(step, _):
            first = 4 * step
            low = high = from_west = from_east = None
            for r in range(3):
                window = padded[pl.ds(first + r, 4)].reshape(4 * COLS, WIDE)
                even, odd = window[:, :HALF], window[:, HALF:]
                terms = (
                    dot(even, sea[r, 1]) + dot(odd, sea[r, 2]),
                    dot(even, sea[r, 0]) + dot(odd, sea[r, 1]),
                    dot(odd, sea[r, 0]),
                    dot(even, sea[r, 2]),
                )
                if low is None:
                    low, high, from_west, from_east = terms
                else:
                    low, high = low + terms[0], high + terms[1]
                    from_west, from_east = from_west + terms[2], from_east + terms[3]
            for i in range(4):
                row = first + i
                part = slice(i * COLS, (i + 1) * COLS)
                old = state[row].astype(F32)
                sides_now = [
                    low[part] + moved(from_west[part], ends[0, pl.ds(row, 1), 0:HALF], 1),
                    high[part] + moved(from_east[part], ends[1, pl.ds(row, 1), 0:HALF], -1),
                ]
                for side in range(2):
                    lanes = slice(side * HALF, (side + 1) * HALF)
                    value = old[:, lanes] + sides_now[side]
                    if forced:
                        given = force[i // 2 + 2 * (step % 2), pl.ds(16 * (step // 2), 16), 16 * (i % 2) : 16 * (i % 2) + 16, :]
                        pick = (cell == 2 * pair + side).astype(F32).astype(BF16)
                        value = value + dot(pick, given.reshape(2 * COLS, HALF))
                    out_ref[row, :, lanes] = (value * water[row, :, side : side + 1]).astype(BF16)
            return 0

        lax.fori_loop(0, 4, some_rows, 0)


def layer_call(layer, forced, state, force, coupling, water, air_kernels, sea_kernels):
    dma = pltpu.SemaphoreType.DMA
    vmem = pl.BlockSpec(memory_space=pltpu.VMEM)
    hbm = pl.BlockSpec(memory_space=pl.ANY)
    return pl.pallas_call(
        partial(layer_kernel, layer, forced),
        out_shape=jax.ShapeDtypeStruct((ROWS, COLS, WIDE), BF16),
        in_specs=[vmem, vmem, vmem, vmem, hbm, hbm],
        out_specs=vmem,
        scratch_shapes=[
            pltpu.VMEM((ROWS + 2, COLS, WIDE), BF16),
            pltpu.VMEM((2, 16, WIDE), BF16),
            pltpu.VMEM((2, 3, 16, WIDE), BF16),
            pltpu.VMEM((2, 24, WIDE), F32),
            pltpu.VMEM((2, 16, WIDE), F32),
            pltpu.VMEM((3, 3, WIDE, WIDE), BF16),
            pltpu.VMEM((3, 3, HALF, HALF), BF16),
            dma,
            dma((8,)),
            dma((8,)),
        ],
        compiler_params=pltpu.CompilerParams(
            collective_id=1 + layer, has_side_effects=True, vmem_limit_bytes=56 << 20
        ),
    )(state, force, coupling, water, air_kernels, sea_kernels)


def body(
    state,
    intersection_lists,
    intersection_matrices,
    water_indicator,
    atmosphere_kernels,
    ocean_kernels,
    flux_projection,
    coupling_matrix,
):
    current = state[0]
    lists = intersection_lists.reshape(3, ENTRIES)
    factors = intersection_matrices.reshape(ENTRIES, BLOCK, BLOCK)
    water = water_indicator.astype(F32).reshape(ROWS, COLS, 2)

    def sea(_):
        halves = [pltpu.VMEM((32, BLOCK, HALF), F32)]
        return payload_call(sea_payloads, 32, halves, lists, current, factors, water)

    def air(_):
        return payload_call(air_payloads, 16, [], lists, current, factors, flux_projection)

    payload, labels = lax.cond(lax.axis_index("grp") == 1, sea, air, 0)
    force = exchange_call(payload, labels)
    for layer in range(LAYERS):
        current = layer_call(
            layer, layer == 0, current, force, coupling_matrix, water, atmosphere_kernels, ocean_kernels
        )
    return current[None]


def solution(mesh):
    placed = (
        P("grp", "lat", "lon", None),
        P("grp", "lat", "lon", None, None),
        P("grp", "lat", "lon", None, None, None),
        P("lat", "lon"),
        P(),
        P(),
        P(),
        P(),
    )
    return jax.shard_map(
        body, mesh=mesh, in_specs=placed, out_specs=P("grp", "lat", "lon", None), check_vma=False
    )
```

time: 535 us -> 187 us (0.35)
  the two profiles are of different devices: /device:TPU:32 before, /device:TPU:1 now
where the time goes in v1:
time: 187 us; the launch traced here: 186 us
  Pallas kernels  178 us (95%)
  local copies, waits for them, and re-layouts  7.12 us (4%)
    pallas_call x1, Pallas kernels, exchange_call(): pl.pallas_call(exchange, out_shape=jax.ShapeDtypeStruct((CHUNKS, 32, PIEC...  120 us
    pallas_call x2, Pallas kernels, layer_call(): pl.pallas_call(partial(layer_kernel, layer, forced), out_shape=jax.ShapeD...  47.5 us
    pallas_call x1, Pallas kernels, payload_call(): pl.pallas_call(kernel, out_shape=(jax.ShapeDtypeStruct((CHUNKS, SLOT_TOTA...  11.2 us
    unnamed x6, local copies, waits for them, and re-layouts  5.1 us

profile of v1, /device:TPU:1, one launch (start us, length us, event | category | flops | bytes accessed | tf_op | source)
XLA Modules:
  0.0 186.4 jit_solution(71759621655884095)
XLA Ops:
  0.0 0.7 convert_element_type.7
  0.7 0.1 copy.10
  0.8 0.7 copy.16
  1.5 11.2 %conditional.1 = ((bf16[4,128,32,256]{3,2,1,0:T(8,128)(2,1)}, s32[1,128]{1,0:T(1,128)S(1)})) conditional(s32[]{:T(128)} %convert_element_type.6, (s32[3,64]{1,0:T(4,128)S(1)}, bf16[16,128,512]{2,1,0:T(8,128)(2,1)}, bf16[64,128,128]{2,1,0:T(8,128)(2,1)}, bf16[512,256]{1,0:T(8,128)(2,1)}) %tuple.23, (s32[3,64]{1,0:T(4,128)S(1)}, ...), branch_computations={%region_0.0_spmd, %region_1.0_spmd} | conditional | bytes 32776 | solution.py:530
  1.5 11.2 %branch_0_fun.1 = (bf16[4,128,32,256]{3,2,1,0:T(8,128)(2,1)}, s32[1,128]{1,0:T(1,128)S(1)}) custom-call(s32[3,64]{1,0:T(4,128)S(1)} %get-tuple-element.21.lists, bf16[16,128,512]{2,1,0:T(8,128)(2,1)} %get-tuple-element.22.state, bf16[64,128,128]{2,1,0:T(8,128)(2,1)} %get-tuple-element.23.factors, bf16[512,256]{1,0:T(8,128)(2,1)} %get-tuple-element.34.projection), custom_call_target="tpu_custom_call" | custom-call | tf_op jit(solution)/shard_map/cond/branch_0_fun/pallas_call | solution.py:103
  12.7 0.0 copy-start.1
  12.7 119.9 %shard_map.83.force = bf16[4,32,32,256]{3,2,1,0:T(8,128)(2,1)S(1)} custom-call(bf16[4,128,32,256]{3,2,1,0:T(8,128)(2,1)} %get-tuple-element.31.payload, s32[1,128]{1,0:T(1,128)S(1)} %get-tuple-element.32.labels), custom_call_target="tpu_custom_call" | custom-call | tf_op jit(solution)/shard_map/pallas_call | solution.py:301
  132.6 0.0 copy-start
  132.6 1.3 copy-done
  133.9 1.9 %copy.12.water = f32[16,128,2]{2,1,0:T(8,128)} copy(f32[16,128,2]{0,2,1:T(2,128)S(1)} %bitcast.14) | data formatting | bytes 32768 | tf_op jit(solution)/shard_map/reshape | solution.py:521
  135.8 0.0 copy-done.1
  135.8 24.0 %shard_map.84.state = bf16[16,128,512]{2,1,0:T(8,128)(2,1)} custom-call(bf16[16,128,512]{2,1,0:T(8,128)(2,1)S(1)} %bitcast.9, bf16[4,32,32,256]{3,2,1,0:T(8,128)(2,1)} %copy-done, bf16[256,512]{1,0:T(8,128)(2,1)} %coupling.3, f32[16,128,2]{2,1,0:T(8,128)} %copy.12.water, bf16[2,3,3,512,512]{4,3,2,1,0:T(8,128)(2,1)} %air_kernels.3, ...), custom_call_target="tpu_custom_call" | custom-call | tf_op jit(solution)/shard_map/pallas_call | solution.py:485
  159.8 23.5 %shard_map.85 = bf16[16,128,512]{2,1,0:T(8,128)(2,1)} custom-call(bf16[16,128,512]{2,1,0:T(8,128)(2,1)} %shard_map.84.state, bf16[4,32,32,256]{3,2,1,0:T(8,128)(2,1)} %copy-done, bf16[256,512]{1,0:T(8,128)(2,1)} %coupling.3, f32[16,128,2]{2,1,0:T(8,128)} %copy.12.water, bf16[2,3,3,512,512]{4,3,2,1,0:T(8,128)(2,1)} %air_kernels.3, ...), custom_call_target="tpu_custom_call" | custom-call | tf_op jit(solution)/shard_map/pallas_call | solution.py:485
  183.3 3.1 %copy.22 = bf16[1,16,128,512]{3,2,1,0:T(8,128)(2,1)} copy(bf16[1,16,128,512]{3,2,1,0:T(8,128)(2,1)} %bitcast.12) | data formatting | bytes 4194304
Async XLA Ops:
  12.7 123.1 %copy-start.1 = (bf16[1,16,128,512]{3,2,1,0:T(8,128)(2,1)S(1)}, bf16[1,16,128,512]{3,2,1,0:T(8,128)(2,1)}, u32[]{:S(2)}) copy-start(bf16[1,16,128,512]{3,2,1,0:T(8,128)(2,1)} %param.10) | copy-start | bytes 6291460
  132.6 1.3 copy-start

commit v2 on v0

v2 whole, which is shorter than its diff:
```python
import jax
import jax.numpy as jnp
from jax import lax
from jax.experimental import pallas as pl
from jax.experimental.pallas import tpu as pltpu
from jax.sharding import PartitionSpec as P

ROWS = 16
COLS = 128
WIDE = 512
HALF = 256
BLOCK = 128
ENTRIES = 64
TILES = 64
SLOT_TOTAL = 2 * TILES
CHUNKS = ((0, 2), (2, 2), (4, 2), (6, 1), (7, 1))
EARLY_CHUNKS = 3
PIECES = tuple(16 * count for _, count in CHUNKS)
N = len(CHUNKS)
MESH = pl.DeviceIdType.MESH
F32 = jnp.float32
BF16 = jnp.bfloat16


def dot(a, b):
    return jnp.dot(a, b, preferred_element_type=F32)


def iota(shape, dim):
    return lax.broadcasted_iota(jnp.int32, shape, dim)


def ones_where(condition):
    return condition.astype(F32).astype(BF16)


def silu(value):
    return value / (1.0 + jnp.exp(-value))


def activated(value):
    return silu(value.astype(F32)).astype(BF16)


def place_entries(lists, labels, places):
    down, across = iota((ENTRIES, ENTRIES), 0), iota((ENTRIES, ENTRIES), 1)

    def column(row):
        return jnp.sum(jnp.where(down == across, row, 0), axis=1, keepdims=True)

    owner_row = lists[0:1, :]
    owner, source, target = column(owner_row), column(lists[1:2, :]), column(lists[2:3, :])
    rank = jnp.sum(((owner_row == owner) & (across < down)).astype(jnp.int32), axis=1, keepdims=True)
    slot = 2 * jnp.bitwise_xor(owner, 8) + rank
    hit = slot == iota((ENTRIES, SLOT_TOTAL), 1)
    entry = jnp.sum(jnp.where(hit, iota((ENTRIES, SLOT_TOTAL), 0), 0), axis=0, keepdims=True)
    taken = jnp.sum(jnp.where(hit, source, 0), axis=0, keepdims=True)
    labels[...] = jnp.sum(jnp.where(hit, target + 1, 0), axis=0, keepdims=True) - 1
    places[...] = jnp.concatenate([entry, taken] * 4, axis=0)


def sort_slots(labels_ref, me, orders):
    labels = labels_ref[...].reshape(TILES, SLOT_TOTAL)
    lane = iota((TILES, SLOT_TOTAL), 1)
    first = jnp.sum(jnp.where(lane == 2 * me, labels, 0), axis=1, keepdims=True)
    second = jnp.sum(jnp.where(lane == 2 * me + 1, labels, 0), axis=1, keepdims=True)
    column = jnp.concatenate([first, second], axis=0)
    down, across = iota((SLOT_TOTAL, SLOT_TOTAL), 0), iota((SLOT_TOTAL, SLOT_TOTAL), 1)
    keys = jnp.broadcast_to(column, (SLOT_TOTAL, SLOT_TOTAL))
    row = jnp.sum(jnp.where(down == across, keys, 0), axis=0, keepdims=True)
    other = jnp.broadcast_to(row, (SLOT_TOTAL, SLOT_TOTAL))
    ahead = (other < keys) | ((other == keys) & (across < down))
    rank = jnp.sum(ahead.astype(jnp.int32), axis=1, keepdims=True)
    hit = rank == across
    slot = 2 * (down % TILES) + down // TILES
    order = jnp.sum(jnp.where(hit, slot, 0), axis=0, keepdims=True)
    sorted_keys = jnp.sum(jnp.where(hit, keys, 0), axis=0, keepdims=True)
    previous = jnp.sum(jnp.where(rank + 1 == across, keys, 0), axis=0, keepdims=True)
    opens = ((sorted_keys != previous) | (iota((1, SLOT_TOTAL), 1) == 0)).astype(jnp.int32)
    count = jnp.sum((keys == across).astype(jnp.int32), axis=0, keepdims=True)
    last = jnp.sum((keys <= across).astype(jnp.int32), axis=0, keepdims=True) - 1
    last = jnp.maximum(last, 0)
    orders[...] = jnp.concatenate([order, opens, last, count] * 2, axis=0)


def air_blocks(state, projection, blocks):
    for row in range(ROWS):
        flux = dot(state[row], projection[...]).astype(BF16)
        band, sub = row // 8, row % 8
        blocks[8 * band : 8 * band + 8, 16 * sub : 16 * sub + 16, :] = flux.reshape(8, 16, HALF)


def sea_blocks(state, water, mask, halves, blocks):
    cell, pair = iota((COLS, 2 * COLS), 1), iota((COLS, 2 * COLS), 0)
    ones = jnp.ones((2 * COLS, HALF), F32).astype(BF16)
    for row in range(ROWS):
        band, sub = row // 8, row % 8
        for side in range(2):
            wet = jnp.where(cell == 2 * pair + side, water[row : row + 1, :], 0).astype(F32).astype(BF16)
            wet = dot(wet, ones)
            lanes = slice(side * HALF, (side + 1) * HALF)
            mask[row, :, lanes] = wet.astype(BF16)
            surface = (state[row, :, lanes].astype(F32) * wet).reshape(16, 8, HALF)
            start = 64 * side + 8 * sub
            for b in range(16):
                halves[4 * (16 * band + b) + start // 32, start % 32 : start % 32 + 8, :] = surface[b]
    cell, place = iota((BLOCK, BLOCK), 0), iota((BLOCK, BLOCK), 1)
    order = ones_where((cell % 2) * 64 + (cell // 16) * 8 + (cell % 16) // 2 == place)

    def one(b, _):
        blocks[b] = dot(order, halves[pl.ds(4 * b, 4)].reshape(BLOCK, HALF).astype(BF16)).astype(BF16)
        return 0

    lax.fori_loop(0, 32, one, 0, unroll=4)


def moved_east(value):
    return jnp.where(iota((COLS, 1), 0) == 0, 0.0, pltpu.roll(value, 1, 0))


def moved_west(value):
    return jnp.where(iota((COLS, 1), 0) == COLS - 1, 0.0, pltpu.roll(value, COLS - 1, 0))


def total(terms):
    result = terms[0]
    for term in terms[1:]:
        result = result + term
    return result


def mix_air(windows, kernel):
    west, here, east = (total([dot(windows[r], kernel[r, tap]) for r in range(3)]) for tap in range(3))
    rows = [slice(i * COLS, (i + 1) * COLS) for i in range(here.shape[0] // COLS)]
    return [here[row] + moved_east(west[row]) + moved_west(east[row]) for row in rows]


def mix_sea(windows, kernel):
    even = [window[:, :HALF] for window in windows]
    odd = [window[:, HALF:] for window in windows]
    low = total([dot(even[r], kernel[r, 1]) + dot(odd[r], kernel[r, 2]) for r in range(3)])
    high = total([dot(even[r], kernel[r, 0]) + dot(odd[r], kernel[r, 1]) for r in range(3)])
    west = total([dot(odd[r], kernel[r, 0]) for r in range(3)])
    east = total([dot(even[r], kernel[r, 2]) for r in range(3)])
    rows = [slice(i * COLS, (i + 1) * COLS) for i in range(low.shape[0] // COLS)]
    return [
        jnp.concatenate([low[row] + moved_east(west[row]), high[row] + moved_west(east[row])], axis=1)
        for row in rows
    ]


def step_kernel(
    lists, state_in, factors_in, water, air_in, sea_in, projection_in, coupling_in, out_ref, *scratch
):
    send, scratch = scratch[:N], scratch[N:]
    recv, scratch = scratch[:N], scratch[N:]
    leaving, scratch = scratch[:N], scratch[N:]
    arriving, scratch = scratch[:N], scratch[N:]
    (state, factors, projection, coupling, air, sea, blocks, mask, sums, acc) = scratch[:10]
    (padded_0, padded_1, edges_0, edges_1, rims_0, rims_1, sides, ends, saved) = scratch[10:19]
    (labels, marks, places, place_table, orders, order_table) = scratch[19:25]
    (fetch, local_sem, own, sent, landed, mark_sem, over_sent, over_landed, rim_sent, rim_landed) = scratch[25:]

    grp, lat, lon = lax.axis_index("grp"), lax.axis_index("lat"), lax.axis_index("lon")
    me = lat * 16 + lon
    high, x, core = lon // 8, (lon // 2) % 4, lon % 2
    facing = (1 - grp, lat, (lon + 8) % 16)
    west, east = (lon + 15) % 16, (lon + 1) % 16
    north, south = (lat + 3) % 4, (lat + 1) % 4

    def target(k):
        z = (lat + k) % 4
        y = (high + k // 16 + k // 2) % 2
        c = (core + k // 32 + k) % 2
        return z, y * 8 + ((x + k // 4 + k) % 4) * 2 + c

    get_state = pltpu.make_async_copy(state_in, state, fetch.at[0])
    get_factors = pltpu.make_async_copy(factors_in, factors, fetch.at[1])
    get_projection = pltpu.make_async_copy(projection_in, projection, fetch.at[2])
    get_coupling = pltpu.make_async_copy(coupling_in, coupling, fetch.at[3])
    get_air = [pltpu.make_async_copy(air_in.at[layer], air, fetch.at[4 + layer]) for layer in range(2)]
    get_sea = [pltpu.make_async_copy(sea_in.at[layer], sea, fetch.at[4 + layer]) for layer in range(2)]
    get_state.start()
    get_projection.start()
    get_factors.start()
    get_coupling.start()

    def on_air(body):
        pl.when(grp == 0)(body)

    def on_sea(body):
        pl.when(grp == 1)(body)

    on_air(get_air[0].start)
    on_sea(get_sea[0].start)

    barrier = pltpu.get_barrier_semaphore()

    def greet(k, _):
        z, j = target(k)
        pl.semaphore_signal(barrier, inc=1, device_id=(grp, z, j), device_id_type=MESH)
        return 0

    lax.fori_loop(1, TILES, greet, 0)
    pl.semaphore_signal(barrier, inc=1, device_id=facing, device_id_type=MESH)

    place_entries(lists, labels, places)
    tell = pltpu.make_async_copy(places, place_table, local_sem.at[0])
    tell.start()

    get_state.wait()
    padded_0[1] = activated(state[0])
    padded_0[16] = activated(state[ROWS - 1])
    for side, first in ((0, 0), (1, COLS - 16)):
        group = silu(state[:, first : first + 16, :].astype(F32))
        edges_0[side] = group[:, 15 * side, :].astype(BF16)

    def rim_copies(layer, padded, edges, rims):
        pushes = [(padded.at[1], padded.at[17], north, lon), (padded.at[16], padded.at[0], south, lon)]
        for side, j in ((0, west), (1, east)):
            for z, place in ((north, 2), (lat, 1), (south, 0)):
                pushes.append((edges.at[side], rims.at[1 - side, place], z, j))
        return [
            pltpu.make_async_remote_copy(
                source,
                goal,
                rim_sent.at[layer, index],
                rim_landed.at[layer, index],
                device_id=(grp, z, j),
                device_id_type=MESH,
            )
            for index, (source, goal, z, j) in enumerate(pushes)
        ]

    first_rims = rim_copies(0, padded_0, edges_0, rims_0)
    pl.semaphore_wait(barrier, TILES)
    for copy in first_rims:
        copy.start()

    def send_label(k, _):
        z, j = target(k)
        pltpu.make_async_remote_copy(
            labels, marks.at[me], mark_sem.at[0], mark_sem.at[1], device_id=(grp, z, j), device_id_type=MESH
        ).start()
        return 0

    lax.fori_loop(1, TILES, send_label, 0)
    own_label = pltpu.make_async_copy(labels, marks.at[me], local_sem.at[1])
    own_label.start()

    @on_air
    def _():
        get_projection.wait()
        air_blocks(state, projection, blocks)

    @on_sea
    def _():
        get_projection.wait()
        sea_blocks(state, water, mask, sums, blocks)

    get_factors.wait()
    tell.wait()

    def write_payloads(chunks):
        start = 16 * CHUNKS[chunks[0]][0]
        length = sum(PIECES[chunk] for chunk in chunks)

        def one(slot, _):
            factor = factors[place_table[0, slot], start : start + length, :]
            value = dot(factor, blocks[place_table[1, slot]]).astype(BF16)
            offset = 0
            for chunk in chunks:
                send[chunk][slot] = value[offset : offset + PIECES[chunk]]
                offset += PIECES[chunk]
            return 0

        lax.fori_loop(0, SLOT_TOTAL, one, 0, unroll=8)

    def own_copy(chunk):
        mine = pl.ds(2 * me, 2)
        return pltpu.make_async_copy(send[chunk].at[mine], recv[chunk].at[mine], own.at[chunk])

    def send_payloads(chunk):
        def one(k, _):
            z, j = target(k)
            pltpu.make_async_remote_copy(
                send[chunk].at[pl.ds(2 * (z * 16 + j), 2)],
                recv[chunk].at[pl.ds(2 * me, 2)],
                sent.at[chunk],
                landed.at[chunk],
                device_id=(grp, z, j),
                device_id_type=MESH,
            ).start()
            return 0

        lax.fori_loop(1, TILES, one, 0)
        own_copy(chunk).start()

    write_payloads((0,))
    send_payloads(0)
    write_payloads(tuple(range(1, N)))
    for chunk in range(1, N):
        send_payloads(chunk)

    def activate(row, _):
        padded_0[row + 1] = activated(state[row])
        return 0

    lax.fori_loop(1, ROWS - 1, activate, 0, unroll=2)
    for copy in first_rims:
        copy.wait()

    def close_rims(padded, rims):
        @pl.when(lat == 0)
        def _():
            padded[0] = jnp.zeros((COLS, WIDE), BF16)

        @pl.when(lat == 3)
        def _():
            padded[17] = jnp.zeros((COLS, WIDE), BF16)

        for side in range(2):
            sides[side, 0:1, :] = rims[side, 0].astype(F32)[15:16] * jnp.where(lat == 0, 0.0, 1.0)
            sides[side, 1:17, :] = rims[side, 1].astype(F32)
            sides[side, 17:18, :] = rims[side, 2].astype(F32)[0:1] * jnp.where(lat == 3, 0.0, 1.0)

    def end_columns():
        @on_air
        def _():
            for side, tap in ((0, 0), (1, 2)):
                ends[side] = total([dot(sides[side, r : r + 16, :].astype(BF16), air[r, tap]) for r in range(3)])

        @on_sea
        def _():
            nothing = jnp.zeros((ROWS, HALF), F32)
            first = total([dot(sides[0, r : r + 16, HALF:].astype(BF16), sea[r, 0]) for r in range(3)])
            final = total([dot(sides[1, r : r + 16, :HALF].astype(BF16), sea[r, 2]) for r in range(3)])
            ends[0] = jnp.concatenate([first, nothing], axis=1)
            ends[1] = jnp.concatenate([nothing, final], axis=1)

    def mixed_rows(mix, kernel):
        def some_rows(step, _):
            windows = [padded_0[pl.ds(4 * step + r, 4)].reshape(4 * COLS, WIDE) for r in range(3)]
            for i, value in enumerate(mix(windows, kernel)):
                acc[4 * step + i] = value + state[4 * step + i].astype(F32)
            return 0

        lax.fori_loop(0, 4, some_rows, 0)

    close_rims(padded_0, rims_0)

    @on_air
    def _():
        get_air[0].wait()
        mixed_rows(mix_air, air)

    @on_sea
    def _():
        get_sea[0].wait()
        mixed_rows(mix_sea, sea)

    end_columns()
    eight = iota((8, 1), 0)

    def add_ends(row, _):
        acc[row, 0:8, :] += jnp.where(eight == 0, ends[0, pl.ds(row, 1), :], 0.0)
        acc[row, COLS - 8 : COLS, :] += jnp.where(eight == 7, ends[1, pl.ds(row, 1), :], 0.0)
        return 0

    lax.fori_loop(0, ROWS, add_ends, 0)
    on_air(get_air[1].start)
    on_sea(get_sea[1].start)
    get_coupling.wait()

    own_label.wait()
    others = pltpu.make_async_remote_copy(
        marks.at[pl.ds(0, TILES - 1)],
        marks.at[pl.ds(0, TILES - 1)],
        mark_sem.at[0],
        mark_sem.at[1],
        device_id=facing,
        device_id_type=MESH,
    )
    others.wait_recv()
    others.wait_send()
    sort_slots(marks, me, orders)
    tell_order = pltpu.make_async_copy(orders, order_table, local_sem.at[2])
    tell_order.start()
    tell_order.wait()

    def crossing(chunk, part):
        half = pl.ds(16 * part, 16)
        return pltpu.make_async_remote_copy(
            leaving[chunk].at[half],
            arriving[chunk].at[half],
            over_sent.at[chunk, part],
            over_landed.at[chunk, part],
            device_id=facing,
            device_id_type=MESH,
        )

    def sum_and_cross(chunk):
        piece = PIECES[chunk]
        own_copy(chunk).wait()
        rest = pl.ds(0, SLOT_TOTAL - 2)
        everyone = pltpu.make_async_remote_copy(
            send[chunk].at[rest],
            recv[chunk].at[rest],
            sent.at[chunk],
            landed.at[chunk],
            device_id=facing,
            device_id_type=MESH,
        )
        everyone.wait_recv()
        everyone.wait_send()

        def accumulate(p, running):
            value = recv[chunk][order_table[0, p]].astype(F32)
            running = jnp.where(order_table[1, p] == 1, 0.0, running) + value
            sums[p, 0:piece, :] = running
            return running

        lax.fori_loop(0, SLOT_TOTAL, accumulate, jnp.zeros((piece, HALF), F32), unroll=8)

        def settle(b, _):
            value = jnp.where(order_table[3, b] > 0, sums[order_table[2, b], 0:piece, :], 0.0)
            leaving[chunk][b] = value.astype(BF16)
            return 0

        lax.fori_loop(0, 32, settle, 0, unroll=4)
        crossing(chunk, 0).start()
        on_air(crossing(chunk, 1).start)

    def finish_rows(chunk):
        crossing(chunk, 0).wait()
        on_air(crossing(chunk, 1).wait_send)
        on_sea(crossing(chunk, 1).wait_recv)
        first, count = CHUNKS[chunk]
        wanted = [(band, i, 8 * band + first + i) for band in range(2) for i in range(count)]

        @on_air
        def _():
            for band, i, row in wanted:
                given = arriving[chunk][8 * band : 8 * band + 8, 16 * i : 16 * i + 16, :]
                value = (acc[row] + dot(given.reshape(COLS, HALF), coupling[...])).astype(BF16)
                state[row] = value
                padded_1[row + 1] = activated(value)

        @on_sea
        def _():
            cell, pair = iota((COLS, 2 * COLS), 1), iota((COLS, 2 * COLS), 0)
            for band, i, row in wanted:
                given = arriving[chunk][16 * band : 16 * band + 16, 16 * i : 16 * i + 16, :]
                given = given.reshape(2 * COLS, HALF)
                parts = [dot(ones_where(cell == 2 * pair + side), given) for side in range(2)]
                value = (acc[row] + jnp.concatenate(parts, axis=1)) * mask[row].astype(F32)
                value = value.astype(BF16)
                state[row] = value
                padded_1[row + 1] = activated(value)

    def last_rows(rows):
        def windows():
            return [jnp.concatenate([padded_1[row + r] for row in rows], axis=0) for r in range(3)]

        @on_air
        def _():
            for row, value in zip(rows, mix_air(windows(), air)):
                value = value + state[row].astype(F32)
                saved[0, row] = value[0:16]
                saved[1, row] = value[COLS - 16 : COLS]
                out_ref[row] = value.astype(BF16)

        @on_sea
        def _():
            for row, value in zip(rows, mix_sea(windows(), sea)):
                value = value + state[row].astype(F32)
                saved[0, row] = value[0:16]
                saved[1, row] = value[COLS - 16 : COLS]
                out_ref[row] = (value * mask[row].astype(F32)).astype(BF16)

    for chunk in range(N):
        sum_and_cross(chunk)
        if 1 <= chunk <= EARLY_CHUNKS:
            finish_rows(chunk - 1)
    on_air(get_air[1].wait)
    on_sea(get_sea[1].wait)
    last_rows((1, 2, 3, 4))
    finish_rows(EARLY_CHUNKS)
    last_rows((9, 10, 11, 12))
    for chunk in range(EARLY_CHUNKS + 1, N):
        finish_rows(chunk)

    for side, first in ((0, 0), (1, COLS - 16)):
        group = padded_1[1:17, first : first + 16, :].astype(F32)
        edges_1[side] = group[:, 15 * side, :].astype(BF16)
    last_rims = rim_copies(1, padded_1, edges_1, rims_1)
    for copy in last_rims:
        copy.start()
    last_rows((5, 6, 7, 8))
    last_rows((13, 14))
    for copy in last_rims:
        copy.wait()
    close_rims(padded_1, rims_1)
    last_rows((0, 15))
    end_columns()
    sixteen = iota((16, 1), 0)

    def patch(row, _):
        left = saved[0, row] + jnp.where(sixteen == 0, ends[0, pl.ds(row, 1), :], 0.0)
        right = saved[1, row] + jnp.where(sixteen == 15, ends[1, pl.ds(row, 1), :], 0.0)

        @on_air
        def _():
            out_ref[row, 0:16, :] = left.astype(BF16)
            out_ref[row, COLS - 16 : COLS, :] = right.astype(BF16)

        @on_sea
        def _():
            out_ref[row, 0:16, :] = (left * mask[row, 0:16, :].astype(F32)).astype(BF16)
            out_ref[row, COLS - 16 : COLS, :] = (right * mask[row, COLS - 16 : COLS, :].astype(F32)).astype(BF16)

        return 0

    lax.fori_loop(0, ROWS, patch, 0)


def body(
    state,
    intersection_lists,
    intersection_matrices,
    water_indicator,
    atmosphere_kernels,
    ocean_kernels,
    flux_projection,
    coupling_matrix,
):
    dma = pltpu.SemaphoreType.DMA
    vmem = pl.BlockSpec(memory_space=pltpu.VMEM)
    hbm = pl.BlockSpec(memory_space=pl.ANY)
    tables = pltpu.VMEM((8, SLOT_TOTAL), jnp.int32)
    scalars = pltpu.SMEM((8, SLOT_TOTAL), jnp.int32)
    slots = [pltpu.VMEM((SLOT_TOTAL, piece, HALF), BF16) for piece in PIECES]
    dense = [pltpu.VMEM((32, piece, HALF), BF16) for piece in PIECES]
    result = pl.pallas_call(
        step_kernel,
        out_shape=jax.ShapeDtypeStruct((ROWS, COLS, WIDE), BF16),
        in_specs=[vmem, hbm, hbm, vmem, hbm, hbm, hbm, hbm],
        out_specs=vmem,
        scratch_shapes=slots
        + slots
        + dense
        + dense
        + [
            pltpu.VMEM((ROWS, COLS, WIDE), BF16),
            pltpu.VMEM((ENTRIES, BLOCK, BLOCK), BF16),
            pltpu.VMEM((WIDE, HALF), BF16),
            pltpu.VMEM((HALF, WIDE), BF16),
            pltpu.VMEM((3, 3, WIDE, WIDE), BF16),
            pltpu.VMEM((3, 3, HALF, HALF), BF16),
            pltpu.VMEM((32, BLOCK, HALF), BF16),
            pltpu.VMEM((ROWS, COLS, WIDE), BF16),
            pltpu.VMEM((SLOT_TOTAL, 32, HALF), F32),
            pltpu.VMEM((ROWS, COLS, WIDE), F32),
            pltpu.VMEM((ROWS + 2, COLS, WIDE), BF16),
            pltpu.VMEM((ROWS + 2, COLS, WIDE), BF16),
            pltpu.VMEM((2, 16, WIDE), BF16),
            pltpu.VMEM((2, 16, WIDE), BF16),
            pltpu.VMEM((2, 3, 16, WIDE), BF16),
            pltpu.VMEM((2, 3, 16, WIDE), BF16),
            pltpu.VMEM((2, 24, WIDE), F32),
            pltpu.VMEM((2, 16, WIDE), F32),
            pltpu.VMEM((2, ROWS, 16, WIDE), F32),
            pltpu.VMEM((1, SLOT_TOTAL), jnp.int32),
            pltpu.VMEM((TILES, 1, SLOT_TOTAL), jnp.int32),
            tables,
            scalars,
            tables,
            scalars,
            dma((6,)),
            dma((3,)),
            dma((N,)),
            dma((N,)),
            dma((N,)),
            dma((2,)),
            dma((N, 2)),
            dma((N, 2)),
            dma((2, 8)),
            dma((2, 8)),
        ],
        compiler_params=pltpu.CompilerParams(
            collective_id=0, has_side_effects=True, vmem_limit_bytes=63 << 20
        ),
    )(
        intersection_lists.reshape(3, ENTRIES),
        state[0],
        intersection_matrices.reshape(ENTRIES, BLOCK, BLOCK),
        water_indicator,
        atmosphere_kernels,
        ocean_kernels,
        flux_projection,
        coupling_matrix,
    )
    return result[None]


def solution(mesh):
    placed = (
        P("grp", "lat", "lon", None),
        P("grp", "lat", "lon", None, None),
        P("grp", "lat", "lon", None, None, None),
        P("lat", "lon"),
        P(),
        P(),
        P(),
        P(),
    )
    return jax.shard_map(
        body, mesh=mesh, in_specs=placed, out_specs=P("grp", "lat", "lon", None), check_vma=False
    )
```

time: 535 us -> 140 us (0.26)
  the two profiles are of different devices: /device:TPU:32 before, /device:TPU:1 now
where the time goes in v2:
time: 140 us; the launch traced here: 139 us
  Pallas kernels  135 us (96%)
  local copies, waits for them, and re-layouts  4.35 us (3%)
    pallas_call x1, Pallas kernels, body(): pl.pallas_call(step_kernel, out_shape=jax.ShapeDtypeStruct((ROWS, COLS, W...  135 us
    unnamed x2, local copies, waits for them, and re-layouts  4.35 us

profile of v2, /device:TPU:1, one launch (start us, length us, event | category | flops | bytes accessed | tf_op | source)
XLA Modules:
  0.0 139.3 jit_solution(13761287387969252597)
XLA Ops:
  0.0 1.3 copy.11
  1.3 135.0 %shard_map.82 = bf16[16,128,512]{2,1,0:T(8,128)(2,1)} custom-call(s32[3,64]{1,0:T(4,128)} %bitcast.9, bf16[16,128,512]{2,1,0:T(8,128)(2,1)} %bitcast.7, bf16[64,128,128]{2,1,0:T(8,128)(2,1)} %bitcast.8, s32[16,256]{1,0:T(8,128)} %water.1, bf16[2,3,3,512,512]{4,3,2,1,0:T(8,128)(2,1)} %air_in.1, bf16[2,3,3,256,256]{4,3,2,1,0:T(8,128)(2,1)} %sea_in.1, ...), custom_call_target="tpu_custom_call" | custom-call | tf_op jit(solution)/shard_map/pallas_call | solution.py:544
  136.2 3.1 %copy.13 = bf16[1,16,128,512]{3,2,1,0:T(8,128)(2,1)} copy(bf16[1,16,128,512]{3,2,1,0:T(8,128)(2,1)} %bitcast.6) | data formatting | bytes 4194304

commit v3 on v2

--- a/solution.py
+++ b/solution.py
@@ -13,9 +13,8 @@
 ENTRIES = 64
 TILES = 64
 SLOT_TOTAL = 2 * TILES
-CHUNKS = ((0, 2), (2, 2), (4, 2), (6, 1), (7, 1))
-EARLY_CHUNKS = 3
-PIECES = tuple(16 * count for _, count in CHUNKS)
+CHUNKS = ((0, 2, 0, 256), (2, 2, 0, 256), (4, 2, 0, 256), (6, 1, 0, 256), (7, 1, 0, 128), (7, 1, 128, 128))
+PIECES = tuple((16 * chunk[1], chunk[3]) for chunk in CHUNKS)
 N = len(CHUNKS)
 MESH = pl.DeviceIdType.MESH
 F32 = jnp.float32
@@ -48,8 +47,8 @@
     def column(row):
         return jnp.sum(jnp.where(down == across, row, 0), axis=1, keepdims=True)
 
-    owner_row = lists[0:1, :]
-    owner, source, target = column(owner_row), column(lists[1:2, :]), column(lists[2:3, :])
+    owner_row = lists[0]
+    owner, source, target = column(owner_row), column(lists[1]), column(lists[2])
     rank = jnp.sum(((owner_row == owner) & (across < down)).astype(jnp.int32), axis=1, keepdims=True)
     slot = 2 * jnp.bitwise_xor(owner, 8) + rank
     hit = slot == iota((ENTRIES, SLOT_TOTAL), 1)
@@ -129,24 +128,45 @@
     return result
 
 
-def mix_air(windows, kernel):
-    west, here, east = (total([dot(windows[r], kernel[r, tap]) for r in range(3)]) for tap in range(3))
-    rows = [slice(i * COLS, (i + 1) * COLS) for i in range(here.shape[0] // COLS)]
-    return [here[row] + moved_east(west[row]) + moved_west(east[row]) for row in rows]
-
-
-def mix_sea(windows, kernel):
+def row_parts(value):
+    return [value[i * COLS : (i + 1) * COLS] for i in range(value.shape[0] // COLS)]
+
+
+def mix_air(windows, kernel, sides=None):
+    left = right = windows
+    if sides is not None:
+        left, right = ([jnp.concatenate(pair, axis=0) for pair in zip(windows, side)] for side in sides)
+    west = total([dot(left[r], kernel[r, 0]) for r in range(3)])
+    here = total([dot(windows[r], kernel[r, 1]) for r in range(3)])
+    east = total([dot(right[r], kernel[r, 2]) for r in range(3)])
+    rows = [a + moved_east(b) + moved_west(c) for a, b, c in zip(*map(row_parts, (here, west, east)))]
+    if sides is None:
+        return rows
+    size = here.shape[0]
+    return rows, (west[size:], east[size:])
+
+
+def mix_sea(windows, kernel, sides=None):
     even = [window[:, :HALF] for window in windows]
     odd = [window[:, HALF:] for window in windows]
+    left, right = odd, even
+    if sides is not None:
+        left = [jnp.concatenate([a, b[:, HALF:]], axis=0) for a, b in zip(odd, sides[0])]
+        right = [jnp.concatenate([a, b[:, :HALF]], axis=0) for a, b in zip(even, sides[1])]
     low = total([dot(even[r], kernel[r, 1]) + dot(odd[r], kernel[r, 2]) for r in range(3)])
     high = total([dot(even[r], kernel[r, 0]) + dot(odd[r], kernel[r, 1]) for r in range(3)])
-    west = total([dot(odd[r], kernel[r, 0]) for r in range(3)])
-    east = total([dot(even[r], kernel[r, 2]) for r in range(3)])
-    rows = [slice(i * COLS, (i + 1) * COLS) for i in range(low.shape[0] // COLS)]
-    return [
-        jnp.concatenate([low[row] + moved_east(west[row]), high[row] + moved_west(east[row])], axis=1)
-        for row in rows
+    west = total([dot(left[r], kernel[r, 0]) for r in range(3)])
+    east = total([dot(right[r], kernel[r, 2]) for r in range(3)])
+    rows = [
+        jnp.concatenate([a + moved_east(c), b + moved_west(d)], axis=1)
+        for a, b, c, d in zip(*map(row_parts, (low, high, west, east)))
     ]
+    if sides is None:
+        return rows
+    size = low.shape[0]
+    nothing = jnp.zeros((ROWS, HALF), F32)
+    ends = jnp.concatenate([west[size:], nothing], axis=1), jnp.concatenate([nothing, east[size:]], axis=1)
+    return rows, ends
 
 
 def step_kernel(
@@ -207,13 +227,6 @@
     place_entries(lists, labels, places)
     tell = pltpu.make_async_copy(places, place_table, local_sem.at[0])
     tell.start()
-
-    get_state.wait()
-    padded_0[1] = activated(state[0])
-    padded_0[16] = activated(state[ROWS - 1])
-    for side, first in ((0, 0), (1, COLS - 16)):
-        group = silu(state[:, first : first + 16, :].astype(F32))
-        edges_0[side] = group[:, 15 * side, :].astype(BF16)
 
     def rim_copies(layer, padded, edges, rims):
         pushes = [(padded.at[1], padded.at[17], north, lon), (padded.at[16], padded.at[0], south, lon)]
@@ -232,10 +245,72 @@
             for index, (source, goal, z, j) in enumerate(pushes)
         ]
 
+    get_state.wait()
+
+    @on_air
+    def _():
+        get_projection.wait()
+        air_blocks(state, projection, blocks)
+
+    @on_sea
+    def _():
+        get_projection.wait()
+        sea_blocks(state, water, mask, sums, blocks)
+
+    get_factors.wait()
+    tell.wait()
+
+    def payload(slot, start, length):
+        factor = factors[place_table[0, slot], start : start + length, :]
+        return dot(factor, blocks[place_table[1, slot]]).astype(BF16)
+
+    def own_copy(chunk):
+        mine = pl.ds(2 * me, 2)
+        return pltpu.make_async_copy(send[chunk].at[mine], recv[chunk].at[mine], own.at[chunk])
+
+    def start_send(chunk, k):
+        z, j = target(k)
+        pltpu.make_async_remote_copy(
+            send[chunk].at[pl.ds(2 * (z * 16 + j), 2)],
+            recv[chunk].at[pl.ds(2 * me, 2)],
+            sent.at[chunk],
+            landed.at[chunk],
+            device_id=(grp, z, j),
+            device_id_type=MESH,
+        ).start()
+
+    def send_payloads(chunk):
+        def one(k, _):
+            start_send(chunk, k)
+            return 0
+
+        lax.fori_loop(1, TILES, one, 0)
+        own_copy(chunk).start()
+
+    def first_payloads(k):
+        z, j = target(k)
+        for i in range(2):
+            slot = 2 * (z * 16 + j) + i
+            send[0][slot] = payload(slot, 0, PIECES[0][0])
+
+    def first_step(k, _):
+        first_payloads(k)
+        start_send(0, k - 1)
+        return 0
+
+    pl.semaphore_wait(barrier, TILES)
+    first_payloads(0)
+    first_payloads(1)
+    lax.fori_loop(2, TILES, first_step, 0, unroll=2)
+    start_send(0, TILES - 1)
+    own_copy(0).start()
+
+    padded_0[1] = activated(state[0])
+    padded_0[16] = activated(state[ROWS - 1])
+    for side, first in ((0, 0), (1, COLS - 16)):
+        group = silu(state[:, first : first + 16, :].astype(F32))
+        edges_0[side] = group[:, 15 * side, :].astype(BF16)
     first_rims = rim_copies(0, padded_0, edges_0, rims_0)
-    pl.semaphore_wait(barrier, TILES)
-    for copy in first_rims:
-        copy.start()
 
     def send_label(k, _):
         z, j = target(k)
@@ -248,57 +323,20 @@
     own_label = pltpu.make_async_copy(labels, marks.at[me], local_sem.at[1])
     own_label.start()
 
-    @on_air
-    def _():
-        get_projection.wait()
-        air_blocks(state, projection, blocks)
-
-    @on_sea
-    def _():
-        get_projection.wait()
-        sea_blocks(state, water, mask, sums, blocks)
-
-    get_factors.wait()
-    tell.wait()
-
-    def write_payloads(chunks):
-        start = 16 * CHUNKS[chunks[0]][0]
-        length = sum(PIECES[chunk] for chunk in chunks)
-
-        def one(slot, _):
-            factor = factors[place_table[0, slot], start : start + length, :]
-            value = dot(factor, blocks[place_table[1, slot]]).astype(BF16)
-            offset = 0
-            for chunk in chunks:
-                send[chunk][slot] = value[offset : offset + PIECES[chunk]]
-                offset += PIECES[chunk]
-            return 0
-
-        lax.fori_loop(0, SLOT_TOTAL, one, 0, unroll=8)
-
-    def own_copy(chunk):
-        mine = pl.ds(2 * me, 2)
-        return pltpu.make_async_copy(send[chunk].at[mine], recv[chunk].at[mine], own.at[chunk])
-
-    def send_payloads(chunk):
-        def one(k, _):
-            z, j = target(k)
-            pltpu.make_async_remote_copy(
-                send[chunk].at[pl.ds(2 * (z * 16 + j), 2)],
-                recv[chunk].at[pl.ds(2 * me, 2)],
-                sent.at[chunk],
-                landed.at[chunk],
-                device_id=(grp, z, j),
-                device_id_type=MESH,
-            ).start()
-            return 0
-
-        lax.fori_loop(1, TILES, one, 0)
-        own_copy(chunk).start()
-
-    write_payloads((0,))
-    send_payloads(0)
-    write_payloads(tuple(range(1, N)))
+    for copy in first_rims:
+        copy.start()
+
+    later = 16 * CHUNKS[1][0]
+
+    def later_payloads(slot, _):
+        value = payload(slot, later, BLOCK - later)
+        for chunk in range(1, N):
+            first, count, lane, lanes = CHUNKS[chunk]
+            start = 16 * first - later
+            send[chunk][slot] = value[start : start + 16 * count, lane : lane + lanes]
+        return 0
+
+    lax.fori_loop(0, SLOT_TOTAL, later_payloads, 0, unroll=8)
     for chunk in range(1, N):
         send_payloads(chunk)
 
@@ -400,7 +438,7 @@
         )
 
     def sum_and_cross(chunk):
-        piece = PIECES[chunk]
+        piece, lanes = PIECES[chunk]
         own_copy(chunk).wait()
         rest = pl.ds(0, SLOT_TOTAL - 2)
         everyone = pltpu.make_async_remote_copy(
@@ -417,13 +455,13 @@
         def accumulate(p, running):
             value = recv[chunk][order_table[0, p]].astype(F32)
             running = jnp.where(order_table[1, p] == 1, 0.0, running) + value
-            sums[p, 0:piece, :] = running
+            sums[p, 0:piece, 0:lanes] = running
             return running
 
-        lax.fori_loop(0, SLOT_TOTAL, accumulate, jnp.zeros((piece, HALF), F32), unroll=8)
+        lax.fori_loop(0, SLOT_TOTAL, accumulate, jnp.zeros((piece, lanes), F32), unroll=8)
 
         def settle(b, _):
-            value = jnp.where(order_table[3, b] > 0, sums[order_table[2, b], 0:piece, :], 0.0)
+            value = jnp.where(order_table[3, b] > 0, sums[order_table[2, b], 0:piece, 0:lanes], 0.0)
             leaving[chunk][b] = value.astype(BF16)
             return 0
 
@@ -431,18 +469,24 @@
         crossing(chunk, 0).start()
         on_air(crossing(chunk, 1).start)
 
-    def finish_rows(chunk):
-        crossing(chunk, 0).wait()
-        on_air(crossing(chunk, 1).wait_send)
-        on_sea(crossing(chunk, 1).wait_recv)
-        first, count = CHUNKS[chunk]
-        wanted = [(band, i, 8 * band + first + i) for band in range(2) for i in range(count)]
+    def finish_rows(*chunks):
+        for chunk in chunks:
+            crossing(chunk, 0).wait()
+            on_air(crossing(chunk, 1).wait_send)
+            on_sea(crossing(chunk, 1).wait_recv)
+        first, count = CHUNKS[chunks[0]][:2]
+        wanted = [(band, i, 8 * band + first + i) for band in (1, 0) for i in range(count)]
+
+        def given(band, i, blocks_across):
+            here = slice(blocks_across * band, blocks_across * (band + 1))
+            parts = [arriving[chunk][here, 16 * i : 16 * i + 16, :] for chunk in chunks]
+            parts = [part.reshape(16 * blocks_across, part.shape[2]) for part in parts]
+            return parts[0] if len(parts) == 1 else jnp.concatenate(parts, axis=1)
 
         @on_air
         def _():
             for band, i, row in wanted:
-                given = arriving[chunk][8 * band : 8 * band + 8, 16 * i : 16 * i + 16, :]
-                value = (acc[row] + dot(given.reshape(COLS, HALF), coupling[...])).astype(BF16)
+                value = (acc[row] + dot(given(band, i, 8), coupling[...])).astype(BF16)
                 state[row] = value
                 padded_1[row + 1] = activated(value)
 
@@ -450,59 +494,71 @@
         def _():
             cell, pair = iota((COLS, 2 * COLS), 1), iota((COLS, 2 * COLS), 0)
             for band, i, row in wanted:
-                given = arriving[chunk][16 * band : 16 * band + 16, 16 * i : 16 * i + 16, :]
-                given = given.reshape(2 * COLS, HALF)
-                parts = [dot(ones_where(cell == 2 * pair + side), given) for side in range(2)]
+                force = given(band, i, 16)
+                parts = [dot(ones_where(cell == 2 * pair + side), force) for side in range(2)]
                 value = (acc[row] + jnp.concatenate(parts, axis=1)) * mask[row].astype(F32)
                 value = value.astype(BF16)
                 state[row] = value
                 padded_1[row + 1] = activated(value)
 
-    def last_rows(rows):
+    def last_rows(rows, closing=False):
         def windows():
             return [jnp.concatenate([padded_1[row + r] for row in rows], axis=0) for r in range(3)]
 
+        def mixed(mix, kernel):
+            if not closing:
+                return mix(windows(), kernel)
+            rims = [[sides[side, r : r + 16, :].astype(BF16) for r in range(3)] for side in range(2)]
+            values, (first, final) = mix(windows(), kernel, rims)
+            ends[0] = first
+            ends[1] = final
+            return values
+
+        def put(row, value, wet):
+            value = value + state[row].astype(F32)
+            saved[0, row] = value[0:16]
+            saved[1, row] = value[COLS - 16 : COLS]
+            out_ref[row] = (value if wet is None else value * wet).astype(BF16)
+
         @on_air
         def _():
-            for row, value in zip(rows, mix_air(windows(), air)):
-                value = value + state[row].astype(F32)
-                saved[0, row] = value[0:16]
-                saved[1, row] = value[COLS - 16 : COLS]
-                out_ref[row] = value.astype(BF16)
+            for row, value in zip(rows, mixed(mix_air, air)):
+                put(row, value, None)
 
         @on_sea
         def _():
-            for row, value in zip(rows, mix_sea(windows(), sea)):
-                value = value + state[row].astype(F32)
-                saved[0, row] = value[0:16]
-                saved[1, row] = value[COLS - 16 : COLS]
-                out_ref[row] = (value * mask[row].astype(F32)).astype(BF16)
-
-    for chunk in range(N):
-        sum_and_cross(chunk)
-        if 1 <= chunk <= EARLY_CHUNKS:
-            finish_rows(chunk - 1)
+            for row, value in zip(rows, mixed(mix_sea, sea)):
+                put(row, value, mask[row].astype(F32))
+
+    last_rims = rim_copies(1, padded_1, edges_1, rims_1)
+    sum_and_cross(0)
+    sum_and_cross(1)
+    finish_rows(0)
+    last_rims[0].start()
+    sum_and_cross(2)
+    finish_rows(1)
+    sum_and_cross(3)
+    finish_rows(2)
     on_air(get_air[1].wait)
     on_sea(get_sea[1].wait)
     last_rows((1, 2, 3, 4))
-    finish_rows(EARLY_CHUNKS)
     last_rows((9, 10, 11, 12))
-    for chunk in range(EARLY_CHUNKS + 1, N):
-        finish_rows(chunk)
-
+    finish_rows(3)
+    sum_and_cross(4)
+    last_rows((5, 13))
+    sum_and_cross(5)
+    finish_rows(4, 5)
+    last_rims[1].start()
     for side, first in ((0, 0), (1, COLS - 16)):
         group = padded_1[1:17, first : first + 16, :].astype(F32)
         edges_1[side] = group[:, 15 * side, :].astype(BF16)
-    last_rims = rim_copies(1, padded_1, edges_1, rims_1)
-    for copy in last_rims:
+    for copy in last_rims[2:]:
         copy.start()
-    last_rows((5, 6, 7, 8))
-    last_rows((13, 14))
+    last_rows((6, 7, 8, 14))
     for copy in last_rims:
         copy.wait()
     close_rims(padded_1, rims_1)
-    last_rows((0, 15))
-    end_columns()
+    last_rows((0, 15), closing=True)
     sixteen = iota((16, 1), 0)
 
     def patch(row, _):
@@ -539,11 +595,11 @@
     hbm = pl.BlockSpec(memory_space=pl.ANY)
     tables = pltpu.VMEM((8, SLOT_TOTAL), jnp.int32)
     scalars = pltpu.SMEM((8, SLOT_TOTAL), jnp.int32)
-    slots = [pltpu.VMEM((SLOT_TOTAL, piece, HALF), BF16) for piece in PIECES]
-    dense = [pltpu.VMEM((32, piece, HALF), BF16) for piece in PIECES]
+    slots = [pltpu.VMEM((SLOT_TOTAL, *piece), BF16) for piece in PIECES]
+    dense = [pltpu.VMEM((32, *piece), BF16) for piece in PIECES]
     result = pl.pallas_call(
         step_kernel,
-        out_shape=jax.ShapeDtypeStruct((ROWS, COLS, WIDE), BF16),
+        out_shape=pltpu.VMEM((ROWS, COLS, WIDE), BF16),
         in_specs=[vmem, hbm, hbm, vmem, hbm, hbm, hbm, hbm],
         out_specs=vmem,
         scratch_shapes=slots
@@ -588,10 +644,10 @@
             dma((2, 8)),
         ],
         compiler_params=pltpu.CompilerParams(
-            collective_id=0, has_side_effects=True, vmem_limit_bytes=63 << 20
+            collective_id=0, has_side_effects=True, vmem_limit_bytes=58 << 20
         ),
     )(
-        intersection_lists.reshape(3, ENTRIES),
+        intersection_lists.reshape(3, 1, ENTRIES),
         state[0],
         intersection_matrices.reshape(ENTRIES, BLOCK, BLOCK),
         water_indicator,

time: 140 us -> 142 us (1.014)
  Pallas kernels: 135 us -> 141 us
  local copies, waits for them, and re-layouts: 4.35 us -> 1.32 us
    pallas_call x1, Pallas kernels: 135 us -> 141 us  [body(): pl.pallas_call(step_kernel, out_shape=pltpu.VMEM((ROWS, COLS, WIDE), BF16...]
    unnamed x2 -> x1, local copies, waits for them, and re-layouts: 4.35 us -> 1.32 us
where the time goes in v3:
time: 142 us
  Pallas kernels  141 us (99%)
    pallas_call x1, Pallas kernels, body(): pl.pallas_call(step_kernel, out_shape=pltpu.VMEM((ROWS, COLS, WIDE), BF16...  141 us

profile of v3, /device:TPU:1, one launch (start us, length us, event | category | flops | bytes accessed | tf_op | source)
XLA Modules:
  0.0 141.9 jit_solution(7798042508685843748)
XLA Ops:
  0.0 140.6 %shard_map.82 = bf16[16,128,512]{2,1,0:T(8,128)(2,1)S(1)} custom-call(s32[3,1,64]{2,1,0:T(1,128)} %bitcast.7, bf16[16,128,512]{2,1,0:T(8,128)(2,1)} %bitcast.5, bf16[64,128,128]{2,1,0:T(8,128)(2,1)} %bitcast.6, s32[16,256]{1,0:T(8,128)} %water.1, bf16[2,3,3,512,512]{4,3,2,1,0:T(8,128)(2,1)} %air_in.1, bf16[2,3,3,256,256]{4,3,2,1,0:T(8,128)(2,1)} %sea_in.1, ...), custom_call_target="tpu_custom_call" | custom-call | tf_op jit(solution)/shard_map/pallas_call | solution.py:600
  140.6 1.3 copy.10

commit v4 on v3

--- a/solution.py
+++ b/solution.py
@@ -13,7 +13,7 @@
 ENTRIES = 64
 TILES = 64
 SLOT_TOTAL = 2 * TILES
-CHUNKS = ((0, 2, 0, 256), (2, 2, 0, 256), (4, 2, 0, 256), (6, 1, 0, 256), (7, 1, 0, 128), (7, 1, 128, 128))
+CHUNKS = tuple((row, 1, 0, 256) for row in range(7)) + ((7, 1, 0, 128), (7, 1, 128, 128))
 PIECES = tuple((16 * chunk[1], chunk[3]) for chunk in CHUNKS)
 N = len(CHUNKS)
 MESH = pl.DeviceIdType.MESH
@@ -298,13 +298,6 @@
         start_send(0, k - 1)
         return 0
 
-    pl.semaphore_wait(barrier, TILES)
-    first_payloads(0)
-    first_payloads(1)
-    lax.fori_loop(2, TILES, first_step, 0, unroll=2)
-    start_send(0, TILES - 1)
-    own_copy(0).start()
-
     padded_0[1] = activated(state[0])
     padded_0[16] = activated(state[ROWS - 1])
     for side, first in ((0, 0), (1, COLS - 16)):
@@ -312,6 +305,7 @@
         edges_0[side] = group[:, 15 * side, :].astype(BF16)
     first_rims = rim_copies(0, padded_0, edges_0, rims_0)
 
+    pl.semaphore_wait(barrier, TILES)
     def send_label(k, _):
         z, j = target(k)
         pltpu.make_async_remote_copy(
@@ -325,6 +319,12 @@
 
     for copy in first_rims:
         copy.start()
+
+    first_payloads(0)
+    first_payloads(1)
+    lax.fori_loop(2, TILES, first_step, 0, unroll=2)
+    start_send(0, TILES - 1)
+    own_copy(0).start()
 
     later = 16 * CHUNKS[1][0]
 
@@ -337,7 +337,7 @@
         return 0
 
     lax.fori_loop(0, SLOT_TOTAL, later_payloads, 0, unroll=8)
-    for chunk in range(1, N):
+    for chunk in range(1, 2):
         send_payloads(chunk)
 
     def activate(row, _):
@@ -437,6 +437,8 @@
             device_id_type=MESH,
         )
 
+    next_sends = [(c + 2,) if c + 2 < N else () for c in range(N)]
+
     def sum_and_cross(chunk):
         piece, lanes = PIECES[chunk]
         own_copy(chunk).wait()
@@ -451,6 +453,8 @@
         )
         everyone.wait_recv()
         everyone.wait_send()
+        for following in next_sends[chunk]:
+            send_payloads(following)
 
         def accumulate(p, running):
             value = recv[chunk][order_table[0, p]].astype(F32)
@@ -535,19 +539,20 @@
     sum_and_cross(1)
     finish_rows(0)
     last_rims[0].start()
-    sum_and_cross(2)
-    finish_rows(1)
-    sum_and_cross(3)
-    finish_rows(2)
+    for chunk in range(2, 6):
+        sum_and_cross(chunk)
+        finish_rows(chunk - 1)
     on_air(get_air[1].wait)
     on_sea(get_sea[1].wait)
+    sum_and_cross(6)
+    finish_rows(5)
     last_rows((1, 2, 3, 4))
+    sum_and_cross(7)
     last_rows((9, 10, 11, 12))
-    finish_rows(3)
-    sum_and_cross(4)
+    sum_and_cross(8)
+    finish_rows(6)
     last_rows((5, 13))
-    sum_and_cross(5)
-    finish_rows(4, 5)
+    finish_rows(7, 8)
     last_rims[1].start()
     for side, first in ((0, 0), (1, COLS - 16)):
         group = padded_1[1:17, first : first + 16, :].astype(F32)

time: 142 us -> 131 us (0.923)
  Pallas kernels: 141 us -> 129 us
    pallas_call x1, Pallas kernels: 141 us -> 129 us  [body(): pl.pallas_call(step_kernel, out_shape=pltpu.VMEM((ROWS, COLS, WIDE), BF16...]
where the time goes in v4:
time: 131 us
  Pallas kernels  129 us (98%)
  local copies, waits for them, and re-layouts  1.32 us (1%)
    pallas_call x1, Pallas kernels, body(): pl.pallas_call(step_kernel, out_shape=pltpu.VMEM((ROWS, COLS, WIDE), BF16...  129 us

profile of v4, /device:TPU:1, one launch (start us, length us, event | category | flops | bytes accessed | tf_op | source)
XLA Modules:
  0.0 130.8 jit_solution(14665900309293136275)
XLA Ops:
  0.0 129.5 %shard_map.82 = bf16[16,128,512]{2,1,0:T(8,128)(2,1)S(1)} custom-call(s32[3,1,64]{2,1,0:T(1,128)} %bitcast.7, bf16[16,128,512]{2,1,0:T(8,128)(2,1)} %bitcast.5, bf16[64,128,128]{2,1,0:T(8,128)(2,1)} %bitcast.6, s32[16,256]{1,0:T(8,128)} %water.1, bf16[2,3,3,512,512]{4,3,2,1,0:T(8,128)(2,1)} %air_in.1, bf16[2,3,3,256,256]{4,3,2,1,0:T(8,128)(2,1)} %sea_in.1, ...), custom_call_target="tpu_custom_call" | custom-call | tf_op jit(solution)/shard_map/pallas_call | solution.py:605
  129.5 1.3 %copy.10 = bf16[1,16,128,512]{3,2,1,0:T(8,128)(2,1)} copy(bf16[1,16,128,512]{3,2,1,0:T(8,128)(2,1)S(1)} %bitcast.4) | data formatting | bytes 4194304

commit v5 on v4

--- a/solution.py
+++ b/solution.py
@@ -13,7 +13,7 @@
 ENTRIES = 64
 TILES = 64
 SLOT_TOTAL = 2 * TILES
-CHUNKS = tuple((row, 1, 0, 256) for row in range(7)) + ((7, 1, 0, 128), (7, 1, 128, 128))
+CHUNKS = tuple((row, 1, 0, 256) for row in (0, 1, 7, 6, 2, 5, 3)) + ((4, 1, 0, 128), (4, 1, 128, 128))
 PIECES = tuple((16 * chunk[1], chunk[3]) for chunk in CHUNKS)
 N = len(CHUNKS)
 MESH = pl.DeviceIdType.MESH
@@ -132,13 +132,16 @@
     return [value[i * COLS : (i + 1) * COLS] for i in range(value.shape[0] // COLS)]
 
 
-def mix_air(windows, kernel, sides=None):
-    left = right = windows
+def mix_air(taps, kernel, sides=None):
+    left = right = taps
     if sides is not None:
-        left, right = ([jnp.concatenate(pair, axis=0) for pair in zip(windows, side)] for side in sides)
-    west = total([dot(left[r], kernel[r, 0]) for r in range(3)])
-    here = total([dot(windows[r], kernel[r, 1]) for r in range(3)])
-    east = total([dot(right[r], kernel[r, 2]) for r in range(3)])
+        left, right = (
+            [(r, jnp.concatenate([window, extra], axis=0)) for (r, window), extra in zip(taps, side)]
+            for side in sides
+        )
+    west = total([dot(window, kernel[r, 0]) for r, window in left])
+    here = total([dot(window, kernel[r, 1]) for r, window in taps])
+    east = total([dot(window, kernel[r, 2]) for r, window in right])
     rows = [a + moved_east(b) + moved_west(c) for a, b, c in zip(*map(row_parts, (here, west, east)))]
     if sides is None:
         return rows
@@ -146,17 +149,17 @@
     return rows, (west[size:], east[size:])
 
 
-def mix_sea(windows, kernel, sides=None):
-    even = [window[:, :HALF] for window in windows]
-    odd = [window[:, HALF:] for window in windows]
+def mix_sea(taps, kernel, sides=None):
+    even = [(r, window[:, :HALF]) for r, window in taps]
+    odd = [(r, window[:, HALF:]) for r, window in taps]
     left, right = odd, even
     if sides is not None:
-        left = [jnp.concatenate([a, b[:, HALF:]], axis=0) for a, b in zip(odd, sides[0])]
-        right = [jnp.concatenate([a, b[:, :HALF]], axis=0) for a, b in zip(even, sides[1])]
-    low = total([dot(even[r], kernel[r, 1]) + dot(odd[r], kernel[r, 2]) for r in range(3)])
-    high = total([dot(even[r], kernel[r, 0]) + dot(odd[r], kernel[r, 1]) for r in range(3)])
-    west = total([dot(left[r], kernel[r, 0]) for r in range(3)])
-    east = total([dot(right[r], kernel[r, 2]) for r in range(3)])
+        left = [(r, jnp.concatenate([a, b[:, HALF:]], axis=0)) for (r, a), b in zip(odd, sides[0])]
+        right = [(r, jnp.concatenate([a, b[:, :HALF]], axis=0)) for (r, a), b in zip(even, sides[1])]
+    low = total([dot(a, kernel[r, 1]) + dot(b, kernel[r, 2]) for (r, a), (_, b) in zip(even, odd)])
+    high = total([dot(a, kernel[r, 0]) + dot(b, kernel[r, 1]) for (r, a), (_, b) in zip(even, odd)])
+    west = total([dot(window, kernel[r, 0]) for r, window in left])
+    east = total([dot(window, kernel[r, 2]) for r, window in right])
     rows = [
         jnp.concatenate([a + moved_east(c), b + moved_west(d)], axis=1)
         for a, b, c, d in zip(*map(row_parts, (low, high, west, east)))
@@ -177,9 +180,9 @@
     leaving, scratch = scratch[:N], scratch[N:]
     arriving, scratch = scratch[:N], scratch[N:]
     (state, factors, projection, coupling, air, sea, blocks, mask, sums, acc) = scratch[:10]
-    (padded_0, padded_1, edges_0, edges_1, rims_0, rims_1, sides, ends, saved) = scratch[10:19]
-    (labels, marks, places, place_table, orders, order_table) = scratch[19:25]
-    (fetch, local_sem, own, sent, landed, mark_sem, over_sent, over_landed, rim_sent, rim_landed) = scratch[25:]
+    (padded_0, padded_1, edges_0, edges_1, corners, rims_0, rims_1, sides, ends, saved, part) = scratch[10:21]
+    (labels, marks, places, place_table, orders, order_table) = scratch[21:27]
+    (fetch, local_sem, own, sent, landed, mark_sem, over_sent, over_landed, rim_sent, rim_landed) = scratch[27:]
 
     grp, lat, lon = lax.axis_index("grp"), lax.axis_index("lat"), lax.axis_index("lon")
     me = lat * 16 + lon
@@ -228,11 +231,12 @@
     tell = pltpu.make_async_copy(places, place_table, local_sem.at[0])
     tell.start()
 
-    def rim_copies(layer, padded, edges, rims):
+    def rim_copies(layer, padded, edges, corners, rims):
         pushes = [(padded.at[1], padded.at[17], north, lon), (padded.at[16], padded.at[0], south, lon)]
         for side, j in ((0, west), (1, east)):
             for z, place in ((north, 2), (lat, 1), (south, 0)):
-                pushes.append((edges.at[side], rims.at[1 - side, place], z, j))
+                source = edges if place == 1 else corners
+                pushes.append((source.at[side], rims.at[1 - side, place], z, j))
         return [
             pltpu.make_async_remote_copy(
                 source,
@@ -291,7 +295,9 @@
         z, j = target(k)
         for i in range(2):
             slot = 2 * (z * 16 + j) + i
-            send[0][slot] = payload(slot, 0, PIECES[0][0])
+            value = payload(slot, 0, 32)
+            send[0][slot] = value[0:16]
+            send[1][slot] = value[16:32]
 
     def first_step(k, _):
         first_payloads(k)
@@ -303,7 +309,7 @@
     for side, first in ((0, 0), (1, COLS - 16)):
         group = silu(state[:, first : first + 16, :].astype(F32))
         edges_0[side] = group[:, 15 * side, :].astype(BF16)
-    first_rims = rim_copies(0, padded_0, edges_0, rims_0)
+    first_rims = rim_copies(0, padded_0, edges_0, edges_0, rims_0)
 
     pl.semaphore_wait(barrier, TILES)
     def send_label(k, _):
@@ -325,20 +331,20 @@
     lax.fori_loop(2, TILES, first_step, 0, unroll=2)
     start_send(0, TILES - 1)
     own_copy(0).start()
-
-    later = 16 * CHUNKS[1][0]
+    send_payloads(1)
+
+    later = 16 * (CHUNKS[1][0] + 1)
 
     def later_payloads(slot, _):
         value = payload(slot, later, BLOCK - later)
-        for chunk in range(1, N):
+        for chunk in range(2, N):
             first, count, lane, lanes = CHUNKS[chunk]
             start = 16 * first - later
             send[chunk][slot] = value[start : start + 16 * count, lane : lane + lanes]
         return 0
 
     lax.fori_loop(0, SLOT_TOTAL, later_payloads, 0, unroll=8)
-    for chunk in range(1, 2):
-        send_payloads(chunk)
+    send_payloads(2)
 
     def activate(row, _):
         padded_0[row + 1] = activated(state[row])
@@ -348,7 +354,7 @@
     for copy in first_rims:
         copy.wait()
 
-    def close_rims(padded, rims):
+    def close_rows(padded):
         @pl.when(lat == 0)
         def _():
             padded[0] = jnp.zeros((COLS, WIDE), BF16)
@@ -357,6 +363,7 @@
         def _():
             padded[17] = jnp.zeros((COLS, WIDE), BF16)
 
+    def close_sides(rims):
         for side in range(2):
             sides[side, 0:1, :] = rims[side, 0].astype(F32)[15:16] * jnp.where(lat == 0, 0.0, 1.0)
             sides[side, 1:17, :] = rims[side, 1].astype(F32)
@@ -379,13 +386,14 @@
     def mixed_rows(mix, kernel):
         def some_rows(step, _):
             windows = [padded_0[pl.ds(4 * step + r, 4)].reshape(4 * COLS, WIDE) for r in range(3)]
-            for i, value in enumerate(mix(windows, kernel)):
+            for i, value in enumerate(mix(list(enumerate(windows)), kernel)):
                 acc[4 * step + i] = value + state[4 * step + i].astype(F32)
             return 0
 
         lax.fori_loop(0, 4, some_rows, 0)
 
-    close_rims(padded_0, rims_0)
+    close_rows(padded_0)
+    close_sides(rims_0)
 
     @on_air
     def _():
@@ -437,7 +445,7 @@
             device_id_type=MESH,
         )
 
-    next_sends = [(c + 2,) if c + 2 < N else () for c in range(N)]
+    next_sends = [(c + 2,) if 0 < c < N - 2 else () for c in range(N)]
 
     def sum_and_cross(chunk):
         piece, lanes = PIECES[chunk]
@@ -505,65 +513,94 @@
                 state[row] = value
                 padded_1[row + 1] = activated(value)
 
-    def last_rows(rows, closing=False):
-        def windows():
-            return [jnp.concatenate([padded_1[row + r] for row in rows], axis=0) for r in range(3)]
-
-        def mixed(mix, kernel):
-            if not closing:
-                return mix(windows(), kernel)
-            rims = [[sides[side, r : r + 16, :].astype(BF16) for r in range(3)] for side in range(2)]
-            values, (first, final) = mix(windows(), kernel, rims)
-            ends[0] = first
-            ends[1] = final
-            return values
-
-        def put(row, value, wet):
-            value = value + state[row].astype(F32)
-            saved[0, row] = value[0:16]
-            saved[1, row] = value[COLS - 16 : COLS]
-            out_ref[row] = (value if wet is None else value * wet).astype(BF16)
-
-        @on_air
-        def _():
-            for row, value in zip(rows, mixed(mix_air, air)):
-                put(row, value, None)
-
-        @on_sea
-        def _():
-            for row, value in zip(rows, mixed(mix_sea, sea)):
-                put(row, value, mask[row].astype(F32))
-
-    last_rims = rim_copies(1, padded_1, edges_1, rims_1)
+    def on_both(body):
+        on_air(lambda: body(mix_air, air, lambda row: None))
+        on_sea(lambda: body(mix_sea, sea, lambda row: mask[row].astype(F32)))
+
+    def put(row, value, wet):
+        value = value + state[row].astype(F32)
+        saved[0, row] = value[0:16]
+        saved[1, row] = value[COLS - 16 : COLS]
+        out_ref[row] = (value if wet is None else value * wet).astype(BF16)
+
+    def window(r, rows):
+        return jnp.concatenate([padded_1[row + r] for row in rows], axis=0)
+
+    def last_rows(rows):
+        def whole(mix, kernel, wet):
+            for row, value in zip(rows, mix([(r, window(r, rows)) for r in range(3)], kernel)):
+                put(row, value, wet(row))
+
+        on_both(whole)
+
+    place_of = {3: 0, 4: 1, 5: 2, 11: 3, 12: 4, 13: 5}
+
+    def some_taps(plan, finished=()):
+        def taps(mix, kernel, wet):
+            found = {}
+            for r, rows in plan:
+                for row, value in zip(rows, mix([(r, window(r, rows))], kernel)):
+                    found.setdefault(row, []).append(value)
+            for row, values in found.items():
+                value = total(values)
+                if plan is not early_taps:
+                    value = value + part[place_of[row]]
+                if row in finished:
+                    put(row, value, wet(row))
+                else:
+                    part[place_of[row]] = value
+
+        on_both(taps)
+
+    early_taps = ((0, (3, 4, 11, 12)), (1, (3, 5, 11, 13)), (2, (4, 5, 12, 13)))
+    late_taps = ((0, (5, 13)), (1, (4, 12)), (2, (3, 11)))
+
+    def take_edges(goal):
+        for side, first in ((0, 0), (1, COLS - 16)):
+            group = padded_1[1:17, first : first + 16, :].astype(F32)
+            goal[side] = group[:, 15 * side, :].astype(BF16)
+
+    last_rims = rim_copies(1, padded_1, edges_1, corners, rims_1)
+    early_rims = [last_rims[index] for index in (0, 1, 2, 4, 5, 7)]
+    late_rims = [last_rims[index] for index in (3, 6)]
+
     sum_and_cross(0)
     sum_and_cross(1)
     finish_rows(0)
-    last_rims[0].start()
-    for chunk in range(2, 6):
-        sum_and_cross(chunk)
-        finish_rows(chunk - 1)
+    sum_and_cross(2)
+    finish_rows(1)
+    sum_and_cross(3)
+    finish_rows(2)
+    take_edges(corners)
+    for copy in early_rims:
+        copy.start()
+    sum_and_cross(4)
+    finish_rows(3)
+    sum_and_cross(5)
+    finish_rows(4)
     on_air(get_air[1].wait)
     on_sea(get_sea[1].wait)
+    last_rows((1, 7, 8, 9))
     sum_and_cross(6)
     finish_rows(5)
-    last_rows((1, 2, 3, 4))
+    for copy in early_rims:
+        copy.wait()
+    close_rows(padded_1)
+    last_rows((0, 6, 14, 15))
     sum_and_cross(7)
-    last_rows((9, 10, 11, 12))
     sum_and_cross(8)
     finish_rows(6)
-    last_rows((5, 13))
+    last_rows((2, 10))
+    some_taps(early_taps)
     finish_rows(7, 8)
-    last_rims[1].start()
-    for side, first in ((0, 0), (1, COLS - 16)):
-        group = padded_1[1:17, first : first + 16, :].astype(F32)
-        edges_1[side] = group[:, 15 * side, :].astype(BF16)
-    for copy in last_rims[2:]:
+    take_edges(edges_1)
+    for copy in late_rims:
         copy.start()
-    last_rows((6, 7, 8, 14))
-    for copy in last_rims:
+    some_taps(late_taps, (3, 4, 5, 11, 12, 13))
+    for copy in late_rims:
         copy.wait()
-    close_rims(padded_1, rims_1)
-    last_rows((0, 15), closing=True)
+    close_sides(rims_1)
+    end_columns()
     sixteen = iota((16, 1), 0)
 
     def patch(row, _):
@@ -626,11 +663,13 @@
             pltpu.VMEM((ROWS + 2, COLS, WIDE), BF16),
             pltpu.VMEM((2, 16, WIDE), BF16),
             pltpu.VMEM((2, 16, WIDE), BF16),
+            pltpu.VMEM((2, 16, WIDE), BF16),
             pltpu.VMEM((2, 3, 16, WIDE), BF16),
             pltpu.VMEM((2, 3, 16, WIDE), BF16),
             pltpu.VMEM((2, 24, WIDE), F32),
             pltpu.VMEM((2, 16, WIDE), F32),
             pltpu.VMEM((2, ROWS, 16, WIDE), F32),
+            pltpu.VMEM((6, COLS, WIDE), F32),
             pltpu.VMEM((1, SLOT_TOTAL), jnp.int32),
             pltpu.VMEM((TILES, 1, SLOT_TOTAL), jnp.int32),
             tables,

time: 131 us -> 129 us (0.985)
    pallas_call x1, Pallas kernels: 129 us -> 128 us  [body(): pl.pallas_call(step_kernel, out_shape=pltpu.VMEM((ROWS, COLS, WIDE), BF16...]
where the time goes in v5:
time: 129 us
  Pallas kernels  128 us (99%)
  local copies, waits for them, and re-layouts  1.32 us (1%)
    pallas_call x1, Pallas kernels, body(): pl.pallas_call(step_kernel, out_shape=pltpu.VMEM((ROWS, COLS, WIDE), BF16...  128 us

profile of v5, /device:TPU:1, one launch (start us, length us, event | category | flops | bytes accessed | tf_op | source)
XLA Modules:
  0.0 129.0 jit_solution(14922499080351031525)
XLA Ops:
  0.0 127.7 %shard_map.82 = bf16[16,128,512]{2,1,0:T(8,128)(2,1)S(1)} custom-call(s32[3,1,64]{2,1,0:T(1,128)} %bitcast.7, bf16[16,128,512]{2,1,0:T(8,128)(2,1)} %bitcast.5, bf16[64,128,128]{2,1,0:T(8,128)(2,1)} %bitcast.6, s32[16,256]{1,0:T(8,128)} %water.1, bf16[2,3,3,512,512]{4,3,2,1,0:T(8,128)(2,1)} %air_in.1, bf16[2,3,3,256,256]{4,3,2,1,0:T(8,128)(2,1)} %sea_in.1, ...), custom_call_target="tpu_custom_call" | custom-call | tf_op jit(solution)/shard_map/pallas_call | solution.py:642
  127.7 1.3 %copy.10 = bf16[1,16,128,512]{3,2,1,0:T(8,128)(2,1)} copy(bf16[1,16,128,512]{3,2,1,0:T(8,128)(2,1)S(1)} %bitcast.4) | data formatting | bytes 4194304
